TPU v7x, 32 devices: a whole 2x2x4 slice. The times are simulated.
32 devices in a mesh: energy: 8 (over z, y), tile: 4 (over x, core).
Axes of the slice: x: 2, y: 2, z: 4, core: 2. Of those that a mesh axis runs over, the one named last changes fastest.
Arguments:
- hamiltonian: float32 [256, 256], replicated, may hold values from -0.8 to 0.8
- onsite: float32 [32, 256], P(('energy', 'tile')), may hold values from 4 to 10
- inject: float32 [32, 256], P(('energy', 'tile')), may hold values from 5 to 50
- phonon_kernel: float32 [32, 32], replicated, may hold values from -1 to 1
- coupling: float32 [16, 9], replicated, may hold values from 0.3 to 1
- neighbours: int32 [16, 8], replicated, may hold values from 0 to 15, as said below
Outputs:
- sigma_blocks: float32 [32, 16, 9, 256], P(('energy', 'tile'))
- density: float32 [32, 256], P(('energy', 'tile'))
Inputs may be any that keep to these rules, and one draw needn't show every extreme that they name: `neighbours`: row t lists 8 distinct tiles, none of them t.
All inputs are finite; a program needn't handle non-finite values.
Results may differ from a plain program's by a relative error of at most 0.0003.
Values sent between devices are 32-bit elements; how exact they have to be, the bound alone decides.
No kernel may reach another device: no remote copies, remote signals or barrier semaphores. Data moves between devices by JAX's collectives and lax.ppermute only.
A program may use at most 64 MiB of HBM per device.

v0:
```python
import jax
import jax.numpy as jnp
from jax import lax
from jax.sharding import PartitionSpec as P

NORB = 256
B = 16
NBR = 8
SWEEPS = 3
ITERS = 2
NT = 16


highest = lax.Precision.HIGHEST


def tile_table(neighbours):
    listed = jnp.concatenate([jnp.arange(NT, dtype=jnp.int32)[:, None], neighbours], axis=1)
    return (listed[:, :, None] == jnp.arange(NT, dtype=jnp.int32)[None, None, :]).astype(
        jnp.float32
    )


def extract(matrix, table):
    grid = matrix.reshape(NT, B, NT, B)
    picked = jnp.einsum("tjm,tamb->abtj", table, grid, precision=highest)
    return picked.reshape(B * B, NT * (NBR + 1))


def assemble(blocks, table):
    blocks_four = blocks.reshape(B, B, NT, NBR + 1)
    grid = jnp.einsum("tjm,abtj->tamb", table, blocks_four, precision=highest)
    return grid.reshape(NORB, NORB)


def green(hamiltonian, table, sigma_flat, onsite_row, inject_row):
    sigma = assemble(sigma_flat, table)
    system = jnp.diag(onsite_row) - hamiltonian - sigma
    inverse = jnp.diag(1.0 / onsite_row)
    for repeat in range(SWEEPS):
        product = jnp.dot(inverse, system, precision=highest, preferred_element_type=jnp.float32)
        inverse = 2.0 * inverse - jnp.dot(
            product, inverse, precision=highest, preferred_element_type=jnp.float32
        )
    source = jnp.diag(inject_row) + sigma
    left = jnp.dot(inverse, source, precision=highest, preferred_element_type=jnp.float32)
    lesser = jnp.dot(left, inverse.T, precision=highest, preferred_element_type=jnp.float32)
    return (extract(lesser, table), jnp.diagonal(lesser))


def local(hamiltonian, onsite, inject, phonon_kernel, coupling, neighbours):
    table = tile_table(neighbours)
    energy_count = lax.axis_size("energy")
    tile_count = lax.axis_size("tile")
    local_energies = onsite.shape[0]
    all_energies = phonon_kernel.shape[0]
    slice_entries = B * B // energy_count
    block_cols = NT * (NBR + 1)
    kernel_six = phonon_kernel.reshape(
        energy_count, tile_count, local_energies, energy_count, tile_count, local_energies
    )
    kernel_both = kernel_six.transpose(1, 0, 2, 4, 3, 5).reshape(all_energies, all_energies)
    coupling_row = coupling.reshape(block_cols)
    green_batch = jax.vmap(green, in_axes=(None, None, 0, 0, 0))
    sigma_local = jnp.zeros((local_energies, B * B, block_cols), jnp.float32)
    density = jnp.zeros((local_energies, NORB), jnp.float32)
    for rounds in range(ITERS):
        lesser_blocks, density = green_batch(hamiltonian, table, sigma_local, onsite, inject)
        spread = lax.all_to_all(lesser_blocks, "energy", split_axis=1, concat_axis=0, tiled=True)
        grouped = lax.all_to_all(spread, "tile", split_axis=2, concat_axis=0, tiled=True)
        mixed = jnp.dot(
            kernel_both,
            grouped.reshape(all_energies, -1),
            precision=highest,
            preferred_element_type=jnp.float32,
        )
        mixed = mixed.reshape(all_energies, slice_entries, block_cols // tile_count)
        returned = lax.all_to_all(mixed, "tile", split_axis=0, concat_axis=2, tiled=True)
        gathered_back = lax.all_to_all(returned, "energy", split_axis=0, concat_axis=1, tiled=True)
        sigma_local = gathered_back * coupling_row[None, None, :]
    sigma_blocks = sigma_local.reshape(local_energies, B * B, NT, NBR + 1).transpose(0, 2, 3, 1)
    return (sigma_blocks, density)


def solution(mesh):
    in_specs = (P(), P(("energy", "tile"), None), P(("energy", "tile"), None), P(), P(), P())
    out_specs = (P(("energy", "tile"), None, None, None), P(("energy", "tile"), None))
    return jax.shard_map(local, mesh=mesh, in_specs=in_specs, out_specs=out_specs, check_vma=False)
```

profile of v0, /device:TPU:0, one launch (start us, length us, event | category | flops | bytes accessed | tf_op | source)
XLA Modules:
  0.0 149.1 jit_solution(13862522693603597136)
XLA Ops:
  0.7 0.7 pad_add_fusion
  1.5 0.5 broadcast.175
  2.0 1.3 reduce.3
  3.4 2.4 %select_add_fusion.1 = (f32[1,16,16,16,16]{3,4,2,1,0:T(8,128)S(1)}, f32[1,16,16,16,16]{3,4,2,1,0:T(8,128)}) fusion(f32[16,16]{1,0:T(8,128)S(1)} %broadcast_in_dim.77, s32[16,16]{0,1:T(8,128)S(1)} %multiply_add_fusion, s32[16,16]{1,0:T(8,128)S(1)} %copy.49, s32[16,9]{1,0:T(8,128)S(1)} %copy.47), kind=kOutput, calls=%fused_computation.2 | convolution fusion | flops 7276800 | bytes 527936 | tf_op jit(solution)/shard_map/vmap(tjm,abtj->tamb)/dot_general | solution.py:32
  5.8 2.9 %copy.48 = f32[1,16,16,16,16]{4,3,2,1,0:T(8,128)} copy(f32[1,16,16,16,16]{3,4,2,1,0:T(8,128)} %get-tuple-element.9) | data formatting | bytes 524288 | tf_op jit(solution)/shard_map/vmap(tjm,abtj->tamb)/transpose | solution.py:32
  8.7 2.5 %reshape.337 = f32[256,256]{1,0:T(8,128)S(1)} reshape(f32[1,16,16,16,16]{4,3,2,1,0:T(8,128)} %copy.48) | data formatting | bytes 524288 | tf_op jit(solution)/shard_map/vmap()/reshape | solution.py:33
  11.8 0.4 convolution_subtract_fusion.5
  13.8 1.9 %copy.50 = f32[1,16,16,16,16]{4,3,2,1,0:T(8,128)} copy(f32[1,16,16,16,16]{3,4,2,1,0:T(8,128)S(1)} %get-tuple-element.8) | data formatting | bytes 524288 | tf_op jit(solution)/shard_map/vmap()/add | solution.py:45
  15.6 2.4 %reshape.358 = f32[256,256,1]{1,0,2:T(8,128)S(1)} reshape(f32[1,16,16,16,16]{4,3,2,1,0:T(8,128)} %copy.50) | data formatting | bytes 524288 | tf_op jit(solution)/shard_map/vmap()/add | solution.py:45
  18.5 1.8 %fusion.43 = f32[16,16,16,16]{3,1,2,0:T(8,128)S(1)} fusion(f32[16,16,256,1]{2,1,3,0:T(8,128)S(1)} %convolution_bitcast_fusion.4, f32[16,16,256,1]{2,1,0,3:T(8,128)S(1)} %bitcast.123), kind=kOutput, calls=%fused_computation.59 | convolution fusion | flops 201326592 | bytes 786432 | tf_op jit(solution)/shard_map/vmap()/dot_general | solution.py:47
  20.3 2.1 %fusion.4 = f32[1,16,16,16,9]{4,2,1,3,0:T(8,128)S(1)} fusion(f32[16,16,16,16]{3,1,2,0:T(8,128)S(1)} %fusion.43, s32[16,9]{1,0:T(8,128)S(1)} %copy.47), kind=kOutput, calls=%fused_computation.9 | convolution fusion | flops 7080192 | bytes 410176 | tf_op jit(solution)/shard_map/vmap(tjm,tamb->abtj)/dot_general | solution.py:26
  22.4 1.8 %copy.52 = f32[1,16,16,16,9]{2,1,4,3,0:T(8,128)S(1)} copy(f32[1,16,16,16,9]{4,2,1,3,0:T(8,128)S(1)} %fusion.4) | data formatting | bytes 294912 | tf_op jit(solution)/shard_map/vmap(tjm,tamb->abtj)/transpose | solution.py:26
  24.2 0.5 reshape.338
  24.8 16.0 %all_to_all.114 = f32[1,256,144]{2,0,1:T(1,128)S(1)} all-to-all(f32[1,256,144]{2,0,1:T(1,128)S(1)} %copy.53), channel_id=1, replica_groups=mesh['energy'=8,'tile'=4] {'energy'}, dimensions={1} | all-to-all | bytes 294912 | tf_op jit(solution)/shard_map/all_to_all | solution.py:69
  41.2 0.9 reshape.373
  42.1 3.5 %all-to-all-start.1 = ((f32[4,1,9216]{2,1,0:T(1,128)}), f32[4,1,9216]{2,1,0:T(1,128)S(1)}, u32[]{:S(2)}, u32[]{:S(2)}) async-start(f32[4,1,9216]{2,1,0:T(1,128)} %reshape.373), calls=%async_computation.1 | async-start | bytes 294912 | tf_op jit(solution)/shard_map/all_to_all | solution.py:70
  46.1 4.1 %all-to-all-done.1 = f32[4,1,9216]{2,1,0:T(1,128)S(1)} async-done(((f32[4,1,9216]{2,1,0:T(1,128)}), f32[4,1,9216]{2,1,0:T(1,128)S(1)}, u32[]{:S(2)}, u32[]{:S(2)}) %all-to-all-start.1) | async-done | bytes 147488 | tf_op jit(solution)/shard_map/all_to_all | solution.py:70
  50.2 0.5 broadcast.176
  50.7 1.0 reduce.4
  52.9 0.6 reshape.342
  53.6 0.6 reshape.375
  54.1 7.1 %all_to_all.115 = f32[4,1,9216]{2,1,0:T(1,128)S(1)} all-to-all(f32[4,1,9216]{2,1,0:T(1,128)S(1)} %reshape.375), channel_id=1, replica_groups=mesh['energy'=8,'tile'=4] {'tile'}, dimensions={0} | all-to-all | bytes 294912 | tf_op jit(solution)/shard_map/all_to_all | solution.py:78
  61.3 1.0 reduce.5
  62.3 0.7 reshape.376
  63.6 12.5 %all_to_all.116 = f32[8,32,144]{2,1,0:T(8,128)S(1)} all-to-all(f32[8,32,144]{2,1,0:T(8,128)S(1)} %all_to_all.92), channel_id=1, replica_groups=mesh['energy'=8,'tile'=4] {'energy'}, dimensions={0} | all-to-all | bytes 294912 | tf_op jit(solution)/shard_map/all_to_all | solution.py:79
  77.1 3.7 %select_add_fusion = (f32[1,16,16,16,16]{3,4,2,1,0:T(8,128)S(1)}, f32[1,16,16,16,16]{3,4,2,1,0:T(8,128)}) fusion(f32[16,16]{1,0:T(8,128)S(1)} %copy-done.6, s32[16,16]{0,1:T(8,128)S(1)} %multiply_add_fusion, s32[16,16]{1,0:T(8,128)S(1)} %copy-done.4, s32[16,9]{1,0:T(8,128)S(1)} %copy.47, f32[16,16,16,9]{1,0,3,2:T(8,128)S(1)} %broadcast_multiply_fusion), kind=kOutput, calls=%fused_computation.1 | convolution fusion | flops 7276800 | bytes 675392 | tf_op jit(solution)/shard_map/vmap(tjm,abtj->tamb)/dot_general | solution.py:32
  80.8 2.9 %copy.61 = f32[1,16,16,16,16]{4,3,2,1,0:T(8,128)} copy(f32[1,16,16,16,16]{3,4,2,1,0:T(8,128)} %get-tuple-element.11) | data formatting | bytes 524288 | tf_op jit(solution)/shard_map/vmap(tjm,abtj->tamb)/transpose | solution.py:32
  83.7 2.5 %reshape.343 = f32[256,256]{1,0:T(8,128)S(1)} reshape(f32[1,16,16,16,16]{4,3,2,1,0:T(8,128)} %copy.61) | data formatting | bytes 524288 | tf_op jit(solution)/shard_map/vmap()/reshape | solution.py:33
  86.7 0.4 convolution_subtract_fusion.2
  88.7 1.9 %copy.62 = f32[1,16,16,16,16]{4,3,2,1,0:T(8,128)} copy(f32[1,16,16,16,16]{3,4,2,1,0:T(8,128)S(1)} %get-tuple-element.10) | data formatting | bytes 524288 | tf_op jit(solution)/shard_map/vmap()/add | solution.py:45
  90.5 2.4 %add.38 = f32[256,256]{1,0:T(8,128)S(1)} reshape(f32[1,16,16,16,16]{4,3,2,1,0:T(8,128)} %copy.62) | data formatting | bytes 524288 | tf_op jit(solution)/shard_map/vmap()/add | solution.py:45
  93.8 2.0 %reshape.344 = f32[16,16,16,16]{3,2,1,0:T(8,128)} reshape(f32[256,256]{1,0:T(8,128)S(1)} %fusion.47) | data formatting | bytes 524288 | tf_op jit(solution)/shard_map/reshape.82
  95.8 3.4 %convolution_bitcast_fusion.2 = f32[1,16,16,16,9]{4,2,1,3,0:T(8,128)S(1)} fusion(f32[16,16,16,16]{3,2,1,0:T(8,128)} %reshape.344, s32[16,9]{1,0:T(8,128)S(1)} %copy.47), kind=kOutput, calls=%fused_computation.11 | convolution fusion | flops 7080192 | bytes 410176 | tf_op jit(solution)/shard_map/vmap(tjm,tamb->abtj)/dot_general | solution.py:26
  99.3 1.8 %copy.64 = f32[1,16,16,16,9]{2,1,4,3,0:T(8,128)S(1)} copy(f32[1,16,16,16,9]{4,2,1,3,0:T(8,128)S(1)} %convolution_bitcast_fusion.2) | data formatting | bytes 294912 | tf_op jit(solution)/shard_map/vmap(tjm,tamb->abtj)/transpose | solution.py:26
  101.0 0.5 reshape.345
  101.7 11.9 %all_to_all.117 = f32[1,256,144]{2,0,1:T(1,128)S(1)} all-to-all(f32[1,256,144]{2,0,1:T(1,128)S(1)} %copy.65), channel_id=1, replica_groups=mesh['energy'=8,'tile'=4] {'energy'}, dimensions={1} | all-to-all | bytes 294912 | tf_op jit(solution)/shard_map/all_to_all | solution.py:69
  114.3 7.1 %all_to_all.118 = f32[4,1,9216]{2,1,0:T(1,128)S(1)} all-to-all(f32[4,1,9216]{2,1,0:T(1,128)S(1)} %reshape.377), channel_id=1, replica_groups=mesh['energy'=8,'tile'=4] {'tile'}, dimensions={0} | all-to-all | bytes 294912 | tf_op jit(solution)/shard_map/all_to_all | solution.py:70
  121.4 1.0 reduce.6
  123.6 0.6 reshape.347
  124.2 0.6 reshape.379
  124.8 7.1 %all_to_all.119 = f32[4,1,9216]{2,1,0:T(1,128)S(1)} all-to-all(f32[4,1,9216]{2,1,0:T(1,128)S(1)} %reshape.379), channel_id=1, replica_groups=mesh['energy'=8,'tile'=4] {'tile'}, dimensions={0} | all-to-all | bytes 294912 | tf_op jit(solution)/shard_map/all_to_all | solution.py:78
  131.9 1.0 reduce.7
  133.0 0.7 reshape.380
  134.0 1.0 all_to_all.103
  135.0 3.6 %all-to-all-start.7 = ((f32[8,32,144]{2,1,0:T(8,128)}), f32[8,32,144]{2,1,0:T(8,128)S(1)}, u32[]{:S(2)}, u32[]{:S(2)}) async-start(f32[8,32,144]{2,1,0:T(8,128)} %all_to_all.103), calls=%async_computation.7 | async-start | bytes 524288 | tf_op jit(solution)/shard_map/all_to_all | solution.py:79
  138.6 2.9 %gather_fusion = f32[256]{0:T(256)} fusion(f32[256,256]{1,0:T(8,128)S(1)} %fusion.47, s32[256]{0:T(256)S(1)} %bitcast.121), kind=kCustom, calls=%fused_computation | custom fusion | bytes 4096 | tf_op jit(solution)/shard_map/vmap(jit(diagonal))/cond/branch_0_fun/gather | solution.py:48
  141.5 6.2 %all-to-all-done.7 = f32[8,32,144]{2,1,0:T(8,128)S(1)} async-done(((f32[8,32,144]{2,1,0:T(8,128)}), f32[8,32,144]{2,1,0:T(8,128)S(1)}, u32[]{:S(2)}, u32[]{:S(2)}) %all-to-all-start.7) | async-done | bytes 147488 | tf_op jit(solution)/shard_map/all_to_all | solution.py:79
  148.3 0.8 copy.71
  (79 shorter events, 11.9 us)
Async XLA Ops:
  1.5 4.3 %copy-start.3 = (s32[16,16]{1,0:T(8,128)}, s32[16,16]{1,0:T(8,128)S(1)}, u32[]{:S(2)}) copy-start(s32[16,16]{1,0:T(8,128)S(1)} %copy.49) | copy-start | bytes 3076
  3.4 2.4 %copy-start.5 = (f32[16,16]{1,0:T(8,128)}, f32[16,16]{1,0:T(8,128)S(1)}, u32[]{:S(2)}) copy-start(f32[16,16]{1,0:T(8,128)S(1)} %broadcast_in_dim.77) | copy-start | bytes 3076
  8.7 2.5 %copy-start.10 = (f32[1,256]{1,0:T(1,128)S(1)}, f32[1,256]{1,0:T(1,128)}, u32[]{:S(2)}) copy-start(f32[1,256]{1,0:T(1,128)} %param.7) | copy-start | bytes 3076
  8.7 2.5 %copy-start = (f32[256,256]{1,0:T(8,128)S(1)}, f32[256,256]{1,0:T(8,128)}, u32[]{:S(2)}) copy-start(f32[256,256]{1,0:T(8,128)} %param.6) | copy-start | bytes 786436
  11.2 2.2 %copy-start.12 = (f32[1,256]{1,0:T(1,128)}, f32[1,256]{1,0:T(1,128)S(1)}, u32[]{:S(2)}) copy-start(f32[1,256]{1,0:T(1,128)S(1)} %broadcast_divide_fusion) | copy-start | bytes 3076
  24.2 21.5 %copy-start.9 = (f32[32,32]{1,0:T(8,128)S(1)}, f32[32,32]{1,0:T(8,128)}, u32[]{:S(2)}) copy-start(f32[32,32]{1,0:T(8,128)} %param.9) | copy-start | bytes 12292
  42.1 8.1 %all-to-all-start.1 = ((f32[4,1,9216]{2,1,0:T(1,128)}), f32[4,1,9216]{2,1,0:T(1,128)S(1)}, u32[]{:S(2)}, u32[]{:S(2)}) async-start(f32[4,1,9216]{2,1,0:T(1,128)} %reshape.373), calls=%async_computation.1 | async-start | bytes 294912 | tf_op jit(solution)/shard_map/all_to_all | solution.py:70
  46.1 7.4 %copy-start.1 = (f32[32,32]{1,0:T(8,128)}, f32[32,32]{1,0:T(8,128)S(1)}, u32[]{:S(2)}) copy-start(f32[32,32]{1,0:T(8,128)S(1)} %reshape.341) | copy-start | bytes 12292
  63.3 13.3 %copy-start.7 = (f32[16,9]{1,0:T(8,128)S(1)}, f32[16,9]{1,0:T(8,128)}, u32[]{:S(2)}) copy-start(f32[16,9]{1,0:T(8,128)} %param.10) | copy-start | bytes 1732
  76.4 0.7 copy-start.4
  76.4 0.7 copy-start.6
  83.7 2.5 %copy-start.11 = (f32[1,256]{1,0:T(1,128)S(1)}, f32[1,256]{1,0:T(1,128)}, u32[]{:S(2)}) copy-start(f32[1,256]{1,0:T(1,128)} %param.7) | copy-start | bytes 3076
  83.7 2.6 %copy-start.13 = (f32[1,256]{1,0:T(1,128)S(1)}, f32[1,256]{1,0:T(1,128)}, u32[]{:S(2)}) copy-start(f32[1,256]{1,0:T(1,128)} %copy-done.12) | copy-start | bytes 3076
  114.2 9.1 %copy-start.2 = (f32[32,32]{1,0:T(8,128)S(1)}, f32[32,32]{1,0:T(8,128)}, u32[]{:S(2)}) copy-start(f32[32,32]{1,0:T(8,128)} %copy-done.1) | copy-start | bytes 12292
  134.0 14.2 %copy-start.8 = (f32[16,9]{1,0:T(8,128)S(1)}, f32[16,9]{1,0:T(8,128)}, u32[]{:S(2)}) copy-start(f32[16,9]{1,0:T(8,128)} %param.10) | copy-start | bytes 1732
  135.0 12.7 %all-to-all-start.7 = ((f32[8,32,144]{2,1,0:T(8,128)}), f32[8,32,144]{2,1,0:T(8,128)S(1)}, u32[]{:S(2)}, u32[]{:S(2)}) async-start(f32[8,32,144]{2,1,0:T(8,128)} %all_to_all.103), calls=%async_computation.7 | async-start | bytes 524288 | tf_op jit(solution)/shard_map/all_to_all | solution.py:79
where the time goes:
time: 150 us; the launch traced here: 149 us
  blocking collectives  61.9 us (41%)
  local copies, waits for them, and re-layouts  42 us (28%)
  matrix products  19.8 us (13%)
  waiting for transfers between devices  10.3 us (7%)
  starting transfers between devices  7.1 us (5%)
  other arithmetic  6.71 us (4%)
    all_to_all x2, blocking collectives, local(): lax.all_to_all(lesser_blocks, 'energy', split_axis=1, concat_axis=0, tile...  28 us
    all_to_all x2, blocking collectives, local(): lax.all_to_all(mixed, 'tile', split_axis=0, concat_axis=2, tiled=True)  14.3 us
    all_to_all x1, blocking collectives, local(): lax.all_to_all(returned, 'energy', split_axis=0, concat_axis=1, tiled=True)  12.5 us
    add x4, local copies, waits for them, and re-layouts, green(): source = jnp.diag(inject_row) + sigma  8.6 us
    all_to_all x1, blocking collectives, local(): lax.all_to_all(spread, 'tile', split_axis=2, concat_axis=0, tiled=True)  7.13 us
    all_to_all x1, waiting for transfers between devices, local(): lax.all_to_all(returned, 'energy', split_axis=0, concat_axis=1, tiled=True)  6.23 us
    dot_general x2, matrix products, assemble(): grid = jnp.einsum('tjm,abtj->tamb', table, blocks_four, precision=highest)  6.07 us
    transpose x2, local copies, waits for them, and re-layouts, assemble(): grid = jnp.einsum('tjm,abtj->tamb', table, blocks_four, precision=highest)  5.76 us
  transfers between devices with their start and end apart: 2, of which 2 were waited for; matrix products, arithmetic and copies ran while one was open for 2% of the time, Pallas kernels for 0%

commit v1 on v0

v1 whole, which is shorter than its diff:
```python
import functools

import jax
import jax.numpy as jnp
from jax import lax
from jax.experimental import pallas as pl
from jax.experimental.pallas import tpu as pltpu
from jax.sharding import PartitionSpec as P

ITERS = 2
LANES = 128
UNROLL = 4

f32 = jnp.float32
VMEM = pl.BlockSpec(memory_space=pltpu.VMEM)
SMEM = pl.BlockSpec(memory_space=pltpu.SMEM)


def split(x):
    high = x.astype(jnp.bfloat16)
    return high, (x - high.astype(f32)).astype(jnp.bfloat16)


def dot3(a, b, dims=((1,), (0,))):
    def one(x, y):
        return lax.dot_general(x, y, (dims, ((), ())), preferred_element_type=f32)

    return one(a[0], b[0]) + (one(a[0], b[1]) + one(a[1], b[0]))


def series(n):
    n1 = split(n)
    square = dot3(n1, n1)
    n2 = split(square)
    cube = dot3(n2, n1)
    fourth = dot3(n2, n2)
    head = n + square + cube
    return head + fourth + dot3(split(fourth), split(head))


def eye(size):
    shape = (size, size)
    return lax.broadcasted_iota(jnp.int32, shape, 0) == lax.broadcasted_iota(jnp.int32, shape, 1)


def first_kernel(place, kernel_ref, levels_ref, h_ref, mine_ref, other_ref, columns):
    norb = h_ref.shape[0]
    half = levels_ref.shape[0] // 2
    me = place[0]
    start = lax.rem(me, 2) * half
    partner = me + 1 - 2 * lax.rem(me, 2)
    groups = columns.shape[0]
    unroll = half // groups
    for g in range(groups):
        rows = jnp.concatenate(
            [levels_ref[start + g * unroll + u, :, :norb] for u in range(unroll)], axis=0
        )
        rows = jnp.concatenate([rows] * (8 // unroll), axis=0) if unroll < 8 else rows
        columns[g, :, : rows.shape[0]] = (1.0 / rows).T
    mine_ref[...] = jnp.zeros_like(mine_ref)
    other_ref[...] = jnp.zeros_like(other_ref)
    diagonal = eye(norb)

    def group(g, carry):
        total_mine = jnp.zeros((norb, norb), f32)
        total_other = jnp.zeros((norb, norb), f32)
        for u in range(unroll):
            e = start + g * unroll + u
            row = levels_ref[e]
            n = h_ref[...] * (1.0 / row[:, :norb])
            s = series(n)
            green = jnp.where(diagonal, 1.0 + s, s) * columns[g, :, u : u + 1]
            lesser = dot3(split(green * row[:, norb:]), split(green), ((1,), (1,)))
            total_mine += kernel_ref[me, e] * lesser
            total_other += kernel_ref[partner, e] * lesser
        mine_ref[...] += total_mine
        other_ref[...] += total_other
        return carry

    lax.fori_loop(0, groups, group, 0)


def second_kernel(
    neighbours, coupling, mine_ref, other_ref, h_ref, onsite_ref, inject_ref, out_ref, density_ref,
    sigma, flat,
):
    norb = h_ref.shape[0]
    tiles, listed = coupling.shape
    b = norb // tiles
    lane_tile = lax.broadcasted_iota(jnp.int32, (1, norb), 1) // b
    for t in range(tiles):
        weight = jnp.where(lane_tile == t, coupling[t, 0], 0.0)
        for j in range(1, listed):
            weight = jnp.where(lane_tile == neighbours[t, j - 1], coupling[t, j], weight)
        rows = pl.ds(t * b, b)
        sigma[rows, :] = (mine_ref[rows, :] + other_ref[rows, :]) * weight
    diagonal = eye(norb)
    inverse_row = 1.0 / onsite_ref[...]
    inverse_column = jnp.broadcast_to(inverse_row, (8, norb)).T[:, :1]
    s = series((h_ref[...] + sigma[...]) * inverse_row)
    green = split(jnp.where(diagonal, 1.0 + s, s) * inverse_column)
    source = jnp.where(diagonal, sigma[...] + inject_ref[...], sigma[...])
    left = dot3(green, split(source))
    lesser = dot3(split(left), green, ((1,), (1,)))
    density_ref[...] = jnp.sum(jnp.where(diagonal, lesser, 0.0), axis=0, keepdims=True)
    sigma[...] = lesser
    flatten(sigma, flat, b)
    per = out_ref.shape[2] // LANES
    for t in range(tiles):
        for j in range(listed):
            m = t if j == 0 else neighbours[t, j - 1]
            for part in range(b * b // LANES):
                r = (t * listed + j) * (b * b // LANES) + part
                out_ref[r // per, :, pl.ds(r % per * LANES, LANES)] = flat[part, t * tiles + m]


def flatten(src, dst, b):
    per = LANES // b
    shape = (per, LANES)
    sub = lax.broadcasted_iota(jnp.int32, shape, 0)
    lane = lax.broadcasted_iota(jnp.int32, shape, 1)
    index = sub * b + lax.rem(lane, b)
    lane_group = lane // b
    norb = src.shape[0]
    for t in range(norb // b):
        for q in range(b // per):
            for h in range(norb // LANES):
                value = None
                for a in range(per):
                    row = src[pl.ds(t * b + q * per + a, 1), pl.ds(h * LANES, LANES)]
                    moved = jnp.take_along_axis(
                        jnp.broadcast_to(row, shape), index, axis=1, mode="promise_in_bounds"
                    )
                    value = moved if value is None else jnp.where(lane_group == a, moved, value)
                dst[q, pl.ds(t * b + h * per, per), 0, :] = value


def mix_kernel(kernel_ref, in_ref, out_ref):
    count = in_ref.shape[0]
    for k in range(in_ref.shape[2] // LANES):
        part = pl.ds(k * LANES, LANES)
        entries = in_ref[:, :, part].reshape(count, LANES)
        mixed = dot3(split(kernel_ref[...]), split(entries))
        out_ref[:, :, part] = mixed.reshape(count, 1, LANES)


def last_kernel(coupling, in_ref, out_ref):
    tiles, listed, size = out_ref.shape
    per = in_ref.shape[2] // LANES
    for t in range(tiles):
        for j in range(listed):
            for part in range(size // LANES):
                r = (t * listed + j) * (size // LANES) + part
                row = in_ref[r // per, :, pl.ds(r % per * LANES, LANES)]
                out_ref[t, pl.ds(j, 1), pl.ds(part * LANES, LANES)] = row * coupling[t, j]


def local(hamiltonian, onsite, inject, phonon_kernel, coupling, neighbours):
    axes = ("energy", "tile")
    tile_count = lax.axis_size("tile")
    count = lax.axis_size("energy") * tile_count
    norb = hamiltonian.shape[0]
    tiles, listed = coupling.shape
    size = (norb // tiles) ** 2
    me = lax.axis_index("energy") * tile_count + lax.axis_index("tile")

    levels = jnp.concatenate([onsite, inject], axis=1)
    levels = jnp.broadcast_to(levels[None], (count, 1, 2 * norb))
    levels = lax.all_to_all(levels, axes, split_axis=0, concat_axis=0, tiled=True)
    half = count // 2
    matrix = jax.ShapeDtypeStruct((norb, norb), f32)
    mine, other = pl.pallas_call(
        first_kernel,
        out_shape=(matrix, matrix),
        in_specs=[SMEM, SMEM, VMEM, VMEM],
        out_specs=(VMEM, VMEM),
        scratch_shapes=[pltpu.VMEM((half // UNROLL, norb, LANES), f32)],
    )(jnp.reshape(me, (1,)).astype(jnp.int32), phonon_kernel, levels, hamiltonian)
    pairs = [(i, i + 1 - 2 * (i % 2)) for i in range(tile_count)]
    other = lax.ppermute(other, "tile", pairs)

    per = -(-tiles * listed * size // (LANES * count))
    pieces = jax.ShapeDtypeStruct((count, 1, per * LANES), f32)
    rows, density = pl.pallas_call(
        second_kernel,
        out_shape=(pieces, jax.ShapeDtypeStruct((1, norb), f32)),
        in_specs=[SMEM, SMEM] + [VMEM] * 5,
        out_specs=(VMEM, VMEM),
        scratch_shapes=[
            pltpu.VMEM((norb, norb), f32),
            pltpu.VMEM((norb // LANES, norb, 1, LANES), f32),
        ],
    )(neighbours, coupling, mine, other, hamiltonian, onsite, inject)
    rows = lax.all_to_all(rows, axes, split_axis=0, concat_axis=0, tiled=True)
    rows = pl.pallas_call(
        mix_kernel, out_shape=pieces, in_specs=[VMEM] * 2, out_specs=VMEM
    )(phonon_kernel, rows)
    rows = lax.all_to_all(rows, axes, split_axis=0, concat_axis=0, tiled=True)
    sigma_blocks = pl.pallas_call(
        last_kernel,
        out_shape=jax.ShapeDtypeStruct((tiles, listed, size), f32),
        in_specs=[SMEM, VMEM],
        out_specs=VMEM,
    )(coupling, rows)
    return sigma_blocks[None], density


def solution(mesh):
    in_specs = (P(), P(("energy", "tile"), None), P(("energy", "tile"), None), P(), P(), P())
    out_specs = (P(("energy", "tile"), None, None, None), P(("energy", "tile"), None))
    return jax.shard_map(local, mesh=mesh, in_specs=in_specs, out_specs=out_specs, check_vma=False)
```

time: 150 us -> 70.8 us (0.47)
  blocking collectives: 61.9 us -> 23.3 us
  local copies, waits for them, and re-layouts: 42 us -> 4.34 us
  Pallas kernels: 0 us -> 25.4 us
  matrix products: 19.8 us -> 0 us
  other arithmetic: 6.71 us -> 0.7 us
  waiting for transfers between devices: 10.3 us -> 8.39 us
    all_to_all x6 -> x2, blocking collectives: 61.9 us -> 23.3 us  [local(): rows = lax.all_to_all(rows, axes, split_axis=0, concat_axis=0, tiled=True)]
    pallas_call x0 -> x4, Pallas kernels: none -> 25.4 us  [the longest x1 17.5 us: local(): pl.pallas_call(first_kernel, out_shape=(matrix, matrix), in_specs=[SMEM,...]
    dot_general x22 -> x0, matrix products: 19.8 us -> none  [the longest x2 6.07 us: assemble(): grid = jnp.einsum('tjm,abtj->tamb', table, blocks_four, precision=highest)]
    transpose x5 -> x0, local copies, waits for them, and re-layouts: 9.61 us -> none  [the longest x2 5.76 us: assemble(): grid = jnp.einsum('tjm,abtj->tamb', table, blocks_four, precision=highest)]
    add x4 -> x0, local copies, waits for them, and re-layouts: 8.6 us -> none  [green(): source = jnp.diag(inject_row) + sigma]
    reshape x12 -> x0, local copies, waits for them, and re-layouts: 8.26 us -> none  [the longest x2 4.95 us: assemble(): return grid.reshape(NORB, NORB)]
    all_to_all x15 -> x0, local copies, waits for them, and re-layouts: 4.73 us -> none  [the longest x4 1.9 us: local(): lax.all_to_all(mixed, 'tile', split_axis=0, concat_axis=2, tiled=True)]
    all_to_all x4 -> x0, other arithmetic: 4.14 us -> none  [the longest x2 2.07 us: local(): lax.all_to_all(mixed, 'tile', split_axis=0, concat_axis=2, tiled=True)]
  transfers between devices with their start and end apart: 2 -> 2, of which waited for: 2 -> 2; matrix products, arithmetic and copies ran while one was open for 2% -> 1% of each run, Pallas kernels for 0% -> 0%
where the time goes in v1:
time: 70.8 us; the launch traced here: 70.3 us
  Pallas kernels  25.4 us (36%)
  blocking collectives  23.3 us (33%)
  waiting for transfers between devices  8.39 us (12%)
  starting transfers between devices  7.44 us (11%)
  local copies, waits for them, and re-layouts  4.34 us (6%)
    all_to_all x2, blocking collectives, local(): rows = lax.all_to_all(rows, axes, split_axis=0, concat_axis=0, tiled=True)  23.3 us
    pallas_call x1, Pallas kernels, local(): pl.pallas_call(first_kernel, out_shape=(matrix, matrix), in_specs=[SMEM,...  17.5 us
    all_to_all x1, waiting for transfers between devices, local(): lax.all_to_all(levels, axes, split_axis=0, concat_axis=0, tiled=True)  7.4 us
    all_to_all x1, starting transfers between devices, local(): lax.all_to_all(levels, axes, split_axis=0, concat_axis=0, tiled=True)  7.33 us
    pallas_call x1, Pallas kernels, local(): pl.pallas_call(second_kernel, out_shape=(pieces, jax.ShapeDtypeStruct((1,...  4.12 us
    unnamed x8, local copies, waits for them, and re-layouts  3.67 us
    pallas_call x1, Pallas kernels, local(): pl.pallas_call(mix_kernel, out_shape=pieces, in_specs=[VMEM] * 2, out_spe...  2.11 us
    pallas_call x1, Pallas kernels, local(): pl.pallas_call(last_kernel, out_shape=jax.ShapeDtypeStruct((tiles, listed...  1.73 us
  transfers between devices with their start and end apart: 2, of which 2 were waited for; matrix products, arithmetic and copies ran while one was open for 1% of the time, Pallas kernels for 0%

profile of v1, /device:TPU:0, one launch (start us, length us, event | category | flops | bytes accessed | tf_op | source)
XLA Modules:
  0.0 70.3 jit_solution(16954957185578970434)
XLA Ops:
  0.6 0.7 pad_maximum_fusion
  1.3 0.7 broadcast_in_dim.12
  2.0 7.3 %all-to-all-start = ((f32[32,1,512]{2,1,0:T(1,128)}), f32[32,1,512]{2,1,0:T(1,128)S(1)}, u32[]{:S(2)}, u32[]{:S(2)}) async-start(f32[32,1,512]{2,1,0:T(1,128)} %broadcast_in_dim.12), calls=%async_computation | async-start | bytes 131072 | tf_op jit(solution)/shard_map/all_to_all | solution.py:169
  9.3 7.4 %all-to-all-done.levels_ref = f32[32,1,512]{2,1,0:T(1,128)S(1)} async-done(((f32[32,1,512]{2,1,0:T(1,128)}), f32[32,1,512]{2,1,0:T(1,128)S(1)}, u32[]{:S(2)}, u32[]{:S(2)}) %all-to-all-start) | async-done | bytes 65568 | tf_op jit(solution)/shard_map/all_to_all | solution.py:169
  16.7 0.0 copy-start.1
  16.7 0.6 copy-done.1
  17.4 0.0 copy-start.2
  17.4 17.5 %shard_map.77 = (f32[256,256]{1,0:T(8,128)}, f32[256,256]{1,0:T(8,128)}) custom-call(s32[1]{0:T(128)} %bitcast.place, f32[32,32]{1,0:T(8,128)} %kernel_ref.3, f32[32,1,512]{2,1,0:T(1,128)} %copy-done.1, f32[256,256]{1,0:T(8,128)} %h_ref.3), custom_call_target="tpu_custom_call" | custom-call | tf_op jit(solution)/shard_map/pallas_call | solution.py:172
  34.9 0.1 collective-permute-start
  35.0 0.0 copy-done.2
  35.0 0.6 copy.8.neighbours
  35.6 1.0 %collective-permute-done.other_ref = f32[256,256]{1,0:T(8,128)S(1)} collective-permute-done((f32[256,256]{1,0:T(8,128)}, f32[256,256]{1,0:T(8,128)S(1)}, u32[]{:S(2)}, u32[]{:S(2)}) %collective-permute-start) | collective-permute-done | bytes 262176 | tf_op jit(solution)/shard_map/ppermute | solution.py:180
  36.6 0.0 copy-start
  36.6 0.7 copy-done
  37.3 4.1 %shard_map.78 = (f32[32,1,1152]{2,1,0:T(1,128)}, f32[1,256]{1,0:T(1,128)}) custom-call(s32[16,8]{1,0:T(8,128)} %copy.8.neighbours, f32[16,9]{1,0:T(8,128)} %coupling.3, f32[256,256]{1,0:T(8,128)} %get-tuple-element.6.mine_ref, f32[256,256]{1,0:T(8,128)} %copy-done, f32[256,256]{1,0:T(8,128)} %h_ref.3, f32[1,256]{1,0:T(1,128)} %onsite_ref.1, f32[1,256]{1,0:T(1,128)} %inject_ref.1), custom_call_target="tpu_custom_call" | custom-call | tf_op jit(solution)/shard_map/pallas_call | solution.py:184
  41.4 11.7 %all_to_all.15.in_ref = f32[32,1,1152]{2,1,0:T(1,128)} all-to-all(f32[32,1,1152]{2,1,0:T(1,128)} %get-tuple-element.8), channel_id=1, replica_groups=mesh['energy'=8,'tile'=4] {'energy','tile'}, dimensions={0} | all-to-all | bytes 294912 | tf_op jit(solution)/shard_map/all_to_all | solution.py:194
  53.1 2.1 %shard_map.79 = f32[32,1,1152]{2,1,0:T(1,128)} custom-call(f32[32,32]{1,0:T(8,128)} %kernel_ref.3, f32[32,1,1152]{2,1,0:T(1,128)} %all_to_all.15.in_ref), custom_call_target="tpu_custom_call" | custom-call | tf_op jit(solution)/shard_map/pallas_call | solution.py:195
  55.2 11.7 %all_to_all.16.in_ref = f32[32,1,1152]{2,1,0:T(1,128)} all-to-all(f32[32,1,1152]{2,1,0:T(1,128)} %shard_map.79), channel_id=1, replica_groups=mesh['energy'=8,'tile'=4] {'energy','tile'}, dimensions={0} | all-to-all | bytes 294912 | tf_op jit(solution)/shard_map/all_to_all | solution.py:198
  66.9 1.7 %shard_map.80 = f32[16,9,256]{2,1,0:T(8,128)} custom-call(f32[16,9]{1,0:T(8,128)} %coupling.3, f32[32,1,1152]{2,1,0:T(1,128)} %all_to_all.16.in_ref), custom_call_target="tpu_custom_call" | custom-call | tf_op jit(solution)/shard_map/pallas_call | solution.py:199
  68.6 1.7 %copy.9 = f32[1,16,9,256]{3,1,2,0:T(8,128)} copy(f32[1,16,9,256]{3,2,1,0:T(8,128)} %bitcast.3) | data formatting | bytes 294912
Async XLA Ops:
  2.0 14.7 %all-to-all-start = ((f32[32,1,512]{2,1,0:T(1,128)}), f32[32,1,512]{2,1,0:T(1,128)S(1)}, u32[]{:S(2)}, u32[]{:S(2)}) async-start(f32[32,1,512]{2,1,0:T(1,128)} %broadcast_in_dim.12), calls=%async_computation | async-start | bytes 131072 | tf_op jit(solution)/shard_map/all_to_all | solution.py:169
  16.7 0.6 copy-start.1
  17.4 17.6 %copy-start.2 = (s32[16,8]{0,1:T(8,128)S(1)}, s32[16,8]{0,1:T(8,128)}, u32[]{:S(2)}) copy-start(s32[16,8]{0,1:T(8,128)} %param.11) | copy-start | bytes 1540
  34.9 1.7 %collective-permute-start = (f32[256,256]{1,0:T(8,128)}, f32[256,256]{1,0:T(8,128)S(1)}, u32[]{:S(2)}, u32[]{:S(2)}) collective-permute-start(f32[256,256]{1,0:T(8,128)} %get-tuple-element.7), channel_id=1, source_target_pairs={{0,1},{1,0},{2,3},{3,2},{4,5},{5,4},{6,7},{7,6},{8,9},{9,8},{10,11... | collective-permute-start | bytes 786440 | tf_op jit(solution)/shard_map/ppermute | solution.py:180
  36.6 0.7 copy-start

commit v2 on v1

v2 whole, which is shorter than its diff:
```python
import jax
import jax.numpy as jnp
from jax import lax
from jax.experimental import pallas as pl
from jax.experimental.pallas import tpu as pltpu
from jax.sharding import PartitionSpec as P

LANES = 128
UNROLL = 4

f32 = jnp.float32
VMEM = pl.BlockSpec(memory_space=pltpu.VMEM)
SMEM = pl.BlockSpec(memory_space=pltpu.SMEM)


def split(x):
    high = x.astype(jnp.bfloat16)
    return high, (x - high.astype(f32)).astype(jnp.bfloat16)


def dot(a, b, dims=((1,), (0,))):
    return lax.dot_general(a, b, (dims, ((), ())), preferred_element_type=f32)


def dot3(a, b, dims=((1,), (0,))):
    return dot(a[0], b[0], dims) + (dot(a[0], b[1], dims) + dot(a[1], b[0], dims))


def each(function, *lists):
    return [function(*items) for items in zip(*lists)]


def series(ns):
    first = each(split, ns)
    squares = each(dot3, first, first)
    second = each(split, squares)
    cubes = each(dot3, second, first)
    heads = each(lambda n, square, cube: n + square + cube, ns, squares, cubes)
    fourths = each(dot3, second, second)
    rests = each(dot3, each(split, fourths), each(split, heads))
    return each(lambda head, fourth, rest: head + fourth + rest, heads, fourths, rests)


def eye(size):
    shape = (size, size)
    return lax.broadcasted_iota(jnp.int32, shape, 0) == lax.broadcasted_iota(jnp.int32, shape, 1)


def call(kernel, out_shape, in_specs, scratch_shapes=(), vmem=8, flops=0):
    count = len(out_shape) if isinstance(out_shape, tuple) else 0
    return pl.pallas_call(
        kernel,
        out_shape=out_shape,
        in_specs=in_specs,
        out_specs=(VMEM,) * count if count else VMEM,
        scratch_shapes=scratch_shapes,
        compiler_params=pltpu.CompilerParams(vmem_limit_bytes=vmem << 20),
        cost_estimate=pl.CostEstimate(flops=flops, bytes_accessed=1 << 18, transcendentals=0),
    )


def levels_kernel(onsite_ref, inject_ref, out_ref):
    count, _, width = out_ref.shape
    norb = width // 2
    out_ref[:, :, :norb] = jnp.broadcast_to(onsite_ref[...].reshape(1, 1, norb), (count, 1, norb))
    out_ref[:, :, norb:] = jnp.broadcast_to(inject_ref[...].reshape(1, 1, norb), (count, 1, norb))


def tables_kernel(listed_t, coupling, weight_ref, lanes_ref):
    tiles, listed = coupling.shape
    norb = weight_ref.shape[0]
    b = norb // tiles
    group = lax.broadcasted_iota(jnp.int32, (b, norb), 1) // b
    slot = lax.broadcasted_iota(jnp.int32, (1, LANES), 1) // b
    for t in range(tiles):
        weight = jnp.where(group == t, coupling[t, 0], 0.0)
        tile = jnp.full((1, LANES), t, jnp.int32)
        for j in range(1, listed):
            m = listed_t[j - 1, t]
            weight = jnp.where(group == m, coupling[t, j], weight)
            tile = jnp.where(slot == j, m, tile)
        weight_ref[pl.ds(t * b, b), :] = weight
        lanes_ref[pl.ds(t, 1), :] = tile


def first_kernel(place, kernel_ref, levels_ref, h_ref, mine_ref, other_ref, columns):
    norb = h_ref.shape[0]
    half = levels_ref.shape[0] // 2
    me = place[0]
    start = lax.rem(me, 2) * half
    partner = me + 1 - 2 * lax.rem(me, 2)
    groups = columns.shape[0]
    unroll = half // groups
    for g in range(groups):
        rows = [levels_ref[start + g * unroll + u % unroll, :, :norb] for u in range(8)]
        columns[g, :, :8] = (1.0 / jnp.concatenate(rows, axis=0)).T
    mine_ref[...] = jnp.zeros_like(mine_ref)
    other_ref[...] = jnp.zeros_like(other_ref)
    diagonal = eye(norb)

    def group(g, carry):
        energies = [start + g * unroll + u for u in range(unroll)]
        rows = [levels_ref[e] for e in energies]
        sums = series([h_ref[...] * (1.0 / row[:, :norb]) for row in rows])
        total_mine = total_other = None
        for u in range(unroll):
            root = jnp.where(diagonal, 1.0 + sums[u], sums[u]) * columns[g, :, u : u + 1]
            high, low = split(root * jnp.sqrt(rows[u][:, norb:]))
            flip = ((1,), (1,))
            part = dot(high, high * jnp.bfloat16(0.5), flip) + dot(high, low, flip)
            mine = kernel_ref[me, energies[u]] * part
            other = kernel_ref[partner, energies[u]] * part
            total_mine = mine if u == 0 else total_mine + mine
            total_other = other if u == 0 else total_other + other
        mine_ref[...] += total_mine
        other_ref[...] += total_other
        return carry

    lax.fori_loop(0, groups, group, 0)


def lesser_function(weight_ref, mine_ref, other_ref, h_ref, onsite_ref, inject_ref):
    norb = h_ref.shape[0]
    total = mine_ref[...] + other_ref[...]
    sigma = (total + total.T) * weight_ref[...]
    diagonal = eye(norb)
    inverse_row = 1.0 / onsite_ref[...]
    inverse_column = jnp.broadcast_to(inverse_row, (8, norb)).T[:, :1]
    (s,) = series([(h_ref[...] + sigma) * inverse_row])
    green = split(jnp.where(diagonal, 1.0 + s, s) * inverse_column)
    source = jnp.where(diagonal, sigma + inject_ref[...], sigma)
    lesser = dot3(split(dot3(green, split(source))), green, ((1,), (1,)))
    return lesser, jnp.sum(jnp.where(diagonal, lesser, 0.0), axis=0, keepdims=True)


def second_kernel(
    listed_t, lanes_ref, weight_ref, mine_ref, other_ref, h_ref, onsite_ref, inject_ref,
    out_ref, density_ref, lesser_ref,
):
    lesser, density_ref[...] = lesser_function(
        weight_ref, mine_ref, other_ref, h_ref, onsite_ref, inject_ref
    )
    lesser_ref[...] = lesser
    norb = lesser_ref.shape[0]
    tiles = lanes_ref.shape[0]
    b = norb // tiles
    last = listed_t.shape[0]
    per = LANES // b
    shape = (per, LANES)
    lane = lax.broadcasted_iota(jnp.int32, shape, 1)
    own = lane // b == lax.broadcasted_iota(jnp.int32, shape, 0)

    def take(values, tile):
        index = lax.rem(tile, per) * b + lax.rem(lane, b)
        return jnp.take_along_axis(values, index, axis=1, mode="promise_in_bounds")

    for t in range(tiles):
        tile = jnp.broadcast_to(lanes_ref[pl.ds(t, 1), :], shape)
        m = listed_t[last - 1, t]
        for part in range(b // per):
            rows = pl.ds(t * b + part * per, per)
            value = take(lesser_ref[rows, :LANES], tile)
            for h in range(1, norb // LANES):
                columns = pl.ds(h * LANES, LANES)
                value = jnp.where(tile // per == h, take(lesser_ref[rows, columns], tile), value)
            columns = pl.ds(pl.multiple_of(m // per * LANES, LANES), LANES)
            block = take(lesser_ref[rows, columns], jnp.full(shape, m, jnp.int32))
            first = (t * (b // per) + part) * (per + 1)
            out_ref[pl.ds(first, per), :] = value
            out_ref[pl.ds(first + per, 1), :] = jnp.sum(
                jnp.where(own, block, 0.0), axis=0, keepdims=True
            )


def mix_kernel(kernel_ref, in_ref, out_ref):
    count = kernel_ref.shape[0]
    stride = in_ref.shape[0] // count
    kernel = split(kernel_ref[...])
    parts = [
        dot3(kernel, split(in_ref[pl.ds(k, count, stride=stride), :])) for k in range(stride)
    ]
    per = stride - 1
    width = LANES // per
    group = lax.broadcasted_iota(jnp.int32, (count, LANES), 1) // width
    step = 1
    while step < per:
        upper = (group // step) % 2 == 1
        for k in range(per):
            if k // step % 2 == 0:
                low, high = parts[k], parts[k + step]
                parts[k] = jnp.where(upper, pltpu.roll(high, step * width, 1), low)
                parts[k + step] = jnp.where(upper, high, pltpu.roll(low, LANES - step * width, 1))
        step *= 2
    for k in range(stride):
        out_ref[pl.ds(k, count, stride=stride), :] = parts[k]


def last_kernel(coupling_ref, in_ref, out_ref):
    listed, tiles, size = out_ref.shape
    parts = size // LANES
    for j in range(listed):
        weight = coupling_ref[:, j : j + 1]
        for part in range(parts):
            rows = in_ref[pl.ds(part * listed + j, tiles, stride=parts * listed), :]
            out_ref[j, :, pl.ds(part * LANES, LANES)] = rows * weight


def row_kernel(
    listed_t, weight_ref, mine_ref, other_ref, h_ref, onsite_ref, inject_ref,
    out_ref, density_ref, lesser_ref, flat,
):
    lesser, density_ref[...] = lesser_function(
        weight_ref, mine_ref, other_ref, h_ref, onsite_ref, inject_ref
    )
    lesser_ref[...] = lesser
    norb = lesser_ref.shape[0]
    listed = listed_t.shape[0] + 1
    tiles = listed_t.shape[1]
    b = norb // tiles
    flatten(lesser_ref, flat, b)
    per = out_ref.shape[2] // LANES
    parts = b * b // LANES
    for t in range(tiles):
        for j in range(listed):
            m = t if j == 0 else listed_t[j - 1, t]
            for part in range(parts):
                r = (t * listed + j) * parts + part
                out_ref[r // per, :, pl.ds(r % per * LANES, LANES)] = flat[part, t * tiles + m]


def flatten(src, dst, b):
    per = LANES // b
    shape = (per, LANES)
    lane = lax.broadcasted_iota(jnp.int32, shape, 1)
    index = lax.broadcasted_iota(jnp.int32, shape, 0) * b + lax.rem(lane, b)
    norb = src.shape[0]
    for t in range(norb // b):
        for q in range(b // per):
            for h in range(norb // LANES):
                value = None
                for a in range(per):
                    row = src[pl.ds(t * b + q * per + a, 1), pl.ds(h * LANES, LANES)]
                    moved = jnp.take_along_axis(
                        jnp.broadcast_to(row, shape), index, axis=1, mode="promise_in_bounds"
                    )
                    value = moved if value is None else jnp.where(lane // b == a, moved, value)
                dst[q, pl.ds(t * b + h * per, per), 0, :] = value


def row_mix_kernel(kernel_ref, in_ref, out_ref):
    count = in_ref.shape[0]
    kernel = split(kernel_ref[...])
    for k in range(in_ref.shape[2] // LANES):
        part = pl.ds(k * LANES, LANES)
        mixed = dot3(kernel, split(in_ref[:, :, part].reshape(count, LANES)))
        out_ref[:, :, part] = mixed.reshape(count, 1, LANES)


def row_last_kernel(coupling, in_ref, out_ref):
    listed, tiles, size = out_ref.shape
    per = in_ref.shape[2] // LANES
    for t in range(tiles):
        for j in range(listed):
            for part in range(size // LANES):
                r = (t * listed + j) * (size // LANES) + part
                row = in_ref[r // per, :, pl.ds(r % per * LANES, LANES)]
                out_ref[j, pl.ds(t, 1), pl.ds(part * LANES, LANES)] = row * coupling[t, j]


def local(hamiltonian, onsite, inject, phonon_kernel, coupling, neighbours):
    axes = ("energy", "tile")
    tile_count = lax.axis_size("tile")
    count = lax.axis_size("energy") * tile_count
    norb = hamiltonian.shape[0]
    tiles, listed = coupling.shape
    b = norb // tiles
    listed_t = neighbours.T

    def array(*shape, dtype=f32):
        return jax.ShapeDtypeStruct(shape, dtype)

    def exchange(x):
        return lax.all_to_all(x, axes, split_axis=0, concat_axis=0, tiled=True)

    levels = call(levels_kernel, array(count, 1, 2 * norb), [VMEM] * 2)(onsite, inject)
    levels = exchange(levels)
    weight, lanes = call(
        tables_kernel,
        (array(norb, norb), array(tiles, LANES, dtype=jnp.int32)),
        [SMEM] * 2,
    )(listed_t, coupling)

    me = lax.axis_index("energy") * tile_count + lax.axis_index("tile")
    half = count // 2
    mine, other = call(
        first_kernel,
        (array(norb, norb),) * 2,
        [SMEM, SMEM, VMEM, VMEM],
        [pltpu.VMEM((half // UNROLL, norb, LANES), f32)],
        vmem=24,
        flops=half * 14 * 2 * norb**3,
    )(jnp.reshape(me, (1,)).astype(jnp.int32), phonon_kernel, levels, hamiltonian)
    other = lax.ppermute(other, "tile", [(i, i + 1 - 2 * (i % 2)) for i in range(tile_count)])

    operands = (weight, mine, other, hamiltonian, onsite, inject)
    green_flops = 18 * 2 * norb**3
    dense = pltpu.VMEM((norb, norb), f32)
    if count * LANES == norb * b and listed * b == LANES + b:
        rows = array(norb * listed * b // LANES, LANES)
        pieces, density = call(
            second_kernel, (rows, array(1, norb)), [SMEM] + [VMEM] * 7, [dense], flops=green_flops
        )(listed_t, lanes, *operands)
        flat = (count, 1, rows.shape[0] * LANES // count)
        pieces = exchange(pieces.reshape(flat)).reshape(rows.shape)
        pieces = call(mix_kernel, rows, [VMEM] * 2)(phonon_kernel, pieces)
        pieces = exchange(pieces.reshape(flat)).reshape(rows.shape)
        blocks = call(last_kernel, array(listed, tiles, b * b), [VMEM] * 2)(coupling, pieces)
    else:
        per = -(-norb * listed * b // (LANES * count))
        rows = array(count, 1, per * LANES)
        pieces, density = call(
            row_kernel,
            (rows, array(1, norb)),
            [SMEM] + [VMEM] * 6,
            [dense, pltpu.VMEM((norb // LANES, norb, 1, LANES), f32)],
            flops=green_flops,
        )(listed_t, *operands)
        pieces = call(row_mix_kernel, rows, [VMEM] * 2)(phonon_kernel, exchange(pieces))
        blocks = call(row_last_kernel, array(listed, tiles, b * b), [SMEM, VMEM])(
            coupling, exchange(pieces)
        )
    return blocks.transpose(1, 0, 2)[None], density


def solution(mesh):
    in_specs = (P(), P(("energy", "tile"), None), P(("energy", "tile"), None), P(), P(), P())
    out_specs = (P(("energy", "tile"), None, None, None), P(("energy", "tile"), None))
    return jax.shard_map(local, mesh=mesh, in_specs=in_specs, out_specs=out_specs, check_vma=False)
```

time: 70.8 us -> 55.8 us (0.79)
  Pallas kernels: 25.4 us -> 16 us
  blocking collectives: 23.3 us -> 20.3 us
  local copies, waits for them, and re-layouts: 4.34 us -> 3 us
    pallas_call x4 -> x6, Pallas kernels: 25.4 us -> 16 us  [the longest x1 10.5 us: local(): call(first_kernel, (array(norb, norb),) * 2, [SMEM, SMEM, VMEM, VMEM], [p...]
    all_to_all x2, blocking collectives: 23.3 us -> 20.3 us  [exchange(): return lax.all_to_all(x, axes, split_axis=0, concat_axis=0, tiled=True)]
    unnamed x8 -> x16, local copies, waits for them, and re-layouts: 3.67 us -> 3 us
  transfers between devices with their start and end apart: 2 -> 2, of which waited for: 2 -> 2; matrix products, arithmetic and copies ran while one was open for 1% -> 0% of each run, Pallas kernels for 0% -> 2%
where the time goes in v2:
time: 55.8 us; the launch traced here: 55.5 us
  blocking collectives  20.3 us (36%)
  Pallas kernels  16 us (29%)
  waiting for transfers between devices  7.94 us (14%)
  starting transfers between devices  7.5 us (13%)
  local copies, waits for them, and re-layouts  3 us (5%)
  between operations  0.69 us (1%)
    all_to_all x2, blocking collectives, exchange(): return lax.all_to_all(x, axes, split_axis=0, concat_axis=0, tiled=True)  20.3 us
    pallas_call x1, Pallas kernels, local(): call(first_kernel, (array(norb, norb),) * 2, [SMEM, SMEM, VMEM, VMEM], [p...  10.5 us
    all_to_all x1, waiting for transfers between devices, exchange(): return lax.all_to_all(x, axes, split_axis=0, concat_axis=0, tiled=True)  7.39 us
    all_to_all x1, starting transfers between devices, exchange(): return lax.all_to_all(x, axes, split_axis=0, concat_axis=0, tiled=True)  7.33 us
    unnamed x16, local copies, waits for them, and re-layouts  3 us
    pallas_call x1, Pallas kernels, local(): call(second_kernel, (rows, array(1, norb)), [SMEM] + [VMEM] * 7, [dense],...  2.84 us
  transfers between devices with their start and end apart: 2, of which 2 were waited for; matrix products, arithmetic and copies ran while one was open for 0% of the time, Pallas kernels for 2%

profile of v2, /device:TPU:0, one launch (start us, length us, event | category | flops | bytes accessed | tf_op | source)
XLA Modules:
  0.0 55.5 jit_solution(12860169167665331205)
XLA Ops:
  0.6 0.0 copy-start.3
  0.6 0.7 %copy-done.3 = f32[1,256]{1,0:T(1,128)S(1)} copy-done((f32[1,256]{1,0:T(1,128)S(1)}, f32[1,256]{1,0:T(1,128)}, u32[]{:S(2)}) %copy-start.3) | copy-done | bytes 1048
  1.3 0.0 copy-start.5
  1.3 0.7 %copy-done.5 = f32[1,256]{1,0:T(1,128)S(1)} copy-done((f32[1,256]{1,0:T(1,128)S(1)}, f32[1,256]{1,0:T(1,128)}, u32[]{:S(2)}) %copy-start.5) | copy-done | bytes 1048
  2.0 0.6 %shard_map.78 = f32[32,1,512]{2,1,0:T(1,128)} custom-call(f32[1,256]{1,0:T(1,128)S(1)} %copy-done.3, f32[1,256]{1,0:T(1,128)S(1)} %copy-done.5), custom_call_target="tpu_custom_call" | custom-call | bytes 262144 | tf_op jit(solution)/shard_map/pallas_call | solution.py:285
  2.6 7.3 %all-to-all-start = ((f32[32,1,512]{2,1,0:T(1,128)}), f32[32,1,512]{2,1,0:T(1,128)S(1)}, u32[]{:S(2)}, u32[]{:S(2)}) async-start(f32[32,1,512]{2,1,0:T(1,128)} %shard_map.78), calls=%async_computation | async-start | bytes 131072 | tf_op jit(solution)/shard_map/all_to_all | solution.py:283
  10.0 0.0 copy-start.1
  10.0 7.4 %all-to-all-done.levels_ref = f32[32,1,512]{2,1,0:T(1,128)S(1)} async-done(((f32[32,1,512]{2,1,0:T(1,128)}), f32[32,1,512]{2,1,0:T(1,128)S(1)}, u32[]{:S(2)}, u32[]{:S(2)}) %all-to-all-start) | async-done | bytes 65568 | tf_op jit(solution)/shard_map/all_to_all | solution.py:283
  17.4 0.0 copy-done.1
  17.4 0.0 copy-start.7
  17.4 0.9 %copy-done.7 = f32[256,256]{1,0:T(8,128)S(1)} copy-done((f32[256,256]{1,0:T(8,128)S(1)}, f32[256,256]{1,0:T(8,128)}, u32[]{:S(2)}) %copy-start.7) | copy-done | bytes 262168
  18.3 0.0 copy-start
  18.3 0.0 copy-start.2
  18.3 0.0 copy-start.6
  18.3 10.5 %shard_map.79 = (f32[256,256]{1,0:T(8,128)S(1)}, f32[256,256]{1,0:T(8,128)S(1)}) custom-call(s32[1]{0:T(128)} %bitcast.1.place, f32[32,32]{1,0:T(8,128)S(1)} %copy-done.1, f32[32,1,512]{2,1,0:T(1,128)S(1)} %all-to-all-done.levels_ref, f32[256,256]{1,0:T(8,128)S(1)} %copy-done.7), custom_call_target="tpu_custom_call" | custom-call | flops 7516192768 | bytes 262144 | tf_op jit(solution)/shard_map/pallas_call | solution.py:295
  28.8 0.2 collective-permute-start
  29.0 0.0 copy-done
  29.0 0.0 copy-done.2
  29.0 0.9 %shard_map.77 = (f32[256,256]{1,0:T(8,128)S(1)}, s32[16,128]{1,0:T(8,128)S(1)}) custom-call(s32[8,16]{1,0:T(8,128)S(1)} %bitcast.13, f32[16,9]{1,0:T(8,128)S(1)} %copy-done), custom_call_target="tpu_custom_call" | custom-call | bytes 262144 | tf_op jit(solution)/shard_map/pallas_call | solution.py:287
  29.9 0.5 collective-permute-done.other_ref
  30.4 0.0 copy-start.4
  30.4 0.0 copy-done.6
  30.4 0.7 %copy-done.4 = f32[1,256]{1,0:T(1,128)S(1)} copy-done((f32[1,256]{1,0:T(1,128)S(1)}, f32[1,256]{1,0:T(1,128)}, u32[]{:S(2)}) %copy-start.4) | copy-done | bytes 1048
  31.1 2.8 %shard_map.80 = (f32[288,128]{1,0:T(8,128)S(1)}, f32[1,256]{1,0:T(1,128)}) custom-call(s32[8,16]{1,0:T(8,128)S(1)} %bitcast.14, s32[16,128]{1,0:T(8,128)S(1)} %get-tuple-element.8.lanes_ref, f32[256,256]{1,0:T(8,128)S(1)} %get-tuple-element.9.weight_ref, f32[256,256]{1,0:T(8,128)S(1)} %get-tuple-element.10.mine_ref, ...), custom_call_target="tpu_custom_call" | custom-call | flops 603979776 | bytes 262144 | tf_op jit(solution)/shard_map/pallas_call | solution.py:310
  34.0 10.1 %all_to_all.15 = f32[32,1,1152]{2,1,0:T(1,128)S(1)} all-to-all(f32[32,1,1152]{2,1,0:T(1,128)S(1)} %bitcast.12), channel_id=1, replica_groups=mesh['energy'=8,'tile'=4] {'energy','tile'}, dimensions={0} | all-to-all | bytes 294912 | tf_op jit(solution)/shard_map/all_to_all | solution.py:283
  44.1 0.4 shard_map.81
  44.5 10.2 %all_to_all.16 = f32[32,1,1152]{2,1,0:T(1,128)S(1)} all-to-all(f32[32,1,1152]{2,1,0:T(1,128)S(1)} %bitcast.10), channel_id=1, replica_groups=mesh['energy'=8,'tile'=4] {'energy','tile'}, dimensions={0} | all-to-all | bytes 294912 | tf_op jit(solution)/shard_map/all_to_all | solution.py:283
  54.7 0.8 %shard_map.82 = f32[9,16,256]{2,1,0:T(8,128)} custom-call(f32[16,9]{1,0:T(8,128)S(1)} %copy-done, f32[288,128]{1,0:T(8,128)S(1)} %bitcast.11), custom_call_target="tpu_custom_call" | custom-call | bytes 262144 | tf_op jit(solution)/shard_map/pallas_call | solution.py:317
Async XLA Ops:
  0.6 0.7 %copy-start.3 = (f32[1,256]{1,0:T(1,128)S(1)}, f32[1,256]{1,0:T(1,128)}, u32[]{:S(2)}) copy-start(f32[1,256]{1,0:T(1,128)} %onsite_ref.3) | copy-start | bytes 3076
  1.3 0.7 %copy-start.5 = (f32[1,256]{1,0:T(1,128)S(1)}, f32[1,256]{1,0:T(1,128)}, u32[]{:S(2)}) copy-start(f32[1,256]{1,0:T(1,128)} %inject_ref.3) | copy-start | bytes 3076
  2.6 14.7 %all-to-all-start = ((f32[32,1,512]{2,1,0:T(1,128)}), f32[32,1,512]{2,1,0:T(1,128)S(1)}, u32[]{:S(2)}, u32[]{:S(2)}) async-start(f32[32,1,512]{2,1,0:T(1,128)} %shard_map.78), calls=%async_computation | async-start | bytes 131072 | tf_op jit(solution)/shard_map/all_to_all | solution.py:283
  10.0 7.4 %copy-start.1 = (f32[32,32]{1,0:T(8,128)S(1)}, f32[32,32]{1,0:T(8,128)}, u32[]{:S(2)}) copy-start(f32[32,32]{1,0:T(8,128)} %kernel_ref.3) | copy-start | bytes 12292
  17.4 1.0 %copy-start.7 = (f32[256,256]{1,0:T(8,128)S(1)}, f32[256,256]{1,0:T(8,128)}, u32[]{:S(2)}) copy-start(f32[256,256]{1,0:T(8,128)} %h_ref.3) | copy-start | bytes 786436
  18.3 10.7 %copy-start = (f32[16,9]{1,0:T(8,128)S(1)}, f32[16,9]{1,0:T(8,128)}, u32[]{:S(2)}) copy-start(f32[16,9]{1,0:T(8,128)} %coupling_ref.1) | copy-start | bytes 1732
  18.3 10.7 %copy-start.2 = (s32[16,8]{0,1:T(8,128)S(1)}, s32[16,8]{0,1:T(8,128)}, u32[]{:S(2)}) copy-start(s32[16,8]{0,1:T(8,128)} %param.11) | copy-start | bytes 1540
  18.3 12.1 %copy-start.6 = (f32[1,256]{1,0:T(1,128)S(1)}, f32[1,256]{1,0:T(1,128)}, u32[]{:S(2)}) copy-start(f32[1,256]{1,0:T(1,128)} %inject_ref.3) | copy-start | bytes 3076
  28.8 1.6 %collective-permute-start = (f32[256,256]{1,0:T(8,128)S(1)}, f32[256,256]{1,0:T(8,128)S(1)}, u32[]{:S(2)}, u32[]{:S(2)}) collective-permute-start(f32[256,256]{1,0:T(8,128)S(1)} %get-tuple-element.11), channel_id=1, source_target_pairs={{0,1},{1,0},{2,3},{3,2},{4,5},{5,4},{6,7},{7,6},{8,9},{9,8},{10,11... | collective-permute-start | bytes 786440 | tf_op jit(solution)/shard_map/ppermute | solution.py:303
  30.4 0.7 %copy-start.4 = (f32[1,256]{1,0:T(1,128)S(1)}, f32[1,256]{1,0:T(1,128)}, u32[]{:S(2)}) copy-start(f32[1,256]{1,0:T(1,128)} %onsite_ref.3) | copy-start | bytes 3076

commit v3 on v2

--- a/solution.py
+++ b/solution.py
@@ -6,11 +6,12 @@
 from jax.sharding import PartitionSpec as P
 
 LANES = 128
-UNROLL = 4
+UNROLL = 5
 
 f32 = jnp.float32
 VMEM = pl.BlockSpec(memory_space=pltpu.VMEM)
 SMEM = pl.BlockSpec(memory_space=pltpu.SMEM)
+HBM = pl.BlockSpec(memory_space=pltpu.HBM)
 
 
 def split(x):
@@ -59,17 +60,48 @@
     )
 
 
-def levels_kernel(onsite_ref, inject_ref, out_ref):
+def levels_kernel(onsite_ref, inject_ref, out_ref, rows, sems):
     count, _, width = out_ref.shape
     norb = width // 2
-    out_ref[:, :, :norb] = jnp.broadcast_to(onsite_ref[...].reshape(1, 1, norb), (count, 1, norb))
-    out_ref[:, :, norb:] = jnp.broadcast_to(inject_ref[...].reshape(1, 1, norb), (count, 1, norb))
-
-
-def tables_kernel(listed_t, coupling, weight_ref, lanes_ref):
+    copies = [
+        pltpu.make_async_copy(ref, rows.at[i], sems.at[i])
+        for i, ref in enumerate((onsite_ref, inject_ref))
+    ]
+    for copy in copies:
+        copy.start()
+    for i, copy in enumerate(copies):
+        copy.wait()
+        out_ref[:, :, pl.ds(i * norb, norb)] = jnp.broadcast_to(rows[i][None], (count, 1, norb))
+
+
+def weighted(h_ref, rows, columns, scales):
+    norb = h_ref.shape[0]
+    diagonal = eye(norb)
+    sums = series([h_ref[...] * (1.0 / row[:, :norb]) for row in rows])
+    totals = [None] * len(scales)
+    for u, row in enumerate(rows):
+        root = jnp.where(diagonal, 1.0 + sums[u], sums[u]) * columns[u]
+        high, low = split(root * jnp.sqrt(row[:, norb:]))
+        flip = ((1,), (1,))
+        part = dot(high, high * jnp.bfloat16(0.5), flip) + dot(high, low, flip)
+        for i, scale in enumerate(scales):
+            totals[i] = scale[u] * part if u == 0 else totals[i] + scale[u] * part
+    return totals
+
+
+def own_kernel(
+    place, listed_t, coupling, kernel_ref, h_ref, levels_ref,
+    weight_ref, lanes_ref, mine_ref, other_ref,
+):
     tiles, listed = coupling.shape
     norb = weight_ref.shape[0]
     b = norb // tiles
+    row = levels_ref[0]
+    column = jnp.broadcast_to(1.0 / row[:, :norb], (8, norb)).T[:, :1]
+    me = place[0]
+    partner = me + 1 - 2 * lax.rem(me, 2)
+    scales = [[kernel_ref[target, me]] for target in (me, partner)]
+    mine_ref[...], other_ref[...] = weighted(h_ref, [row], [column], scales)
     group = lax.broadcasted_iota(jnp.int32, (b, norb), 1) // b
     slot = lax.broadcasted_iota(jnp.int32, (1, LANES), 1) // b
     for t in range(tiles):
@@ -83,62 +115,68 @@
         lanes_ref[pl.ds(t, 1), :] = tile
 
 
-def first_kernel(place, kernel_ref, levels_ref, h_ref, mine_ref, other_ref, columns):
+def first_kernel(
+    place, kernel_ref, levels_ref, h_ref, own_mine_ref, own_other_ref,
+    mine_ref, other_ref, columns,
+):
     norb = h_ref.shape[0]
     half = levels_ref.shape[0] // 2
     me = place[0]
-    start = lax.rem(me, 2) * half
-    partner = me + 1 - 2 * lax.rem(me, 2)
+    parity = lax.rem(me, 2)
+    partner = me + 1 - 2 * parity
     groups = columns.shape[0]
-    unroll = half // groups
+    unroll = -(-(half - 1) // groups)
+
+    def energy(k):
+        return 2 * lax.rem(me // 2 + jnp.minimum(k, half - 1), half) + parity
+
+    def fill(g):
+        rows = [levels_ref[energy(1 + g * unroll + u % unroll), :, :norb] for u in range(8)]
+        columns[g, :, :8] = (1.0 / jnp.concatenate(rows, axis=0)).T
+
     for g in range(groups):
-        rows = [levels_ref[start + g * unroll + u % unroll, :, :norb] for u in range(8)]
-        columns[g, :, :8] = (1.0 / jnp.concatenate(rows, axis=0)).T
-    mine_ref[...] = jnp.zeros_like(mine_ref)
-    other_ref[...] = jnp.zeros_like(other_ref)
-    diagonal = eye(norb)
+        fill(g)
+    mine_ref[...] = own_mine_ref[...]
+    other_ref[...] = own_other_ref[...]
 
     def group(g, carry):
-        energies = [start + g * unroll + u for u in range(unroll)]
-        rows = [levels_ref[e] for e in energies]
-        sums = series([h_ref[...] * (1.0 / row[:, :norb]) for row in rows])
-        total_mine = total_other = None
-        for u in range(unroll):
-            root = jnp.where(diagonal, 1.0 + sums[u], sums[u]) * columns[g, :, u : u + 1]
-            high, low = split(root * jnp.sqrt(rows[u][:, norb:]))
-            flip = ((1,), (1,))
-            part = dot(high, high * jnp.bfloat16(0.5), flip) + dot(high, low, flip)
-            mine = kernel_ref[me, energies[u]] * part
-            other = kernel_ref[partner, energies[u]] * part
-            total_mine = mine if u == 0 else total_mine + mine
-            total_other = other if u == 0 else total_other + other
-        mine_ref[...] += total_mine
-        other_ref[...] += total_other
+        ks = [1 + g * unroll + u for u in range(unroll)]
+        rows = [levels_ref[energy(k)] for k in ks]
+        scales = [
+            [jnp.where(k < half, kernel_ref[target, energy(k)], 0.0) for k in ks]
+            for target in (me, partner)
+        ]
+        mine, other = weighted(
+            h_ref, rows, [columns[g, :, u : u + 1] for u in range(unroll)], scales
+        )
+        mine_ref[...] += mine
+        other_ref[...] += other
         return carry
 
     lax.fori_loop(0, groups, group, 0)
 
 
-def lesser_function(weight_ref, mine_ref, other_ref, h_ref, onsite_ref, inject_ref):
+def lesser_function(place, weight_ref, mine_ref, other_ref, h_ref, levels_ref):
     norb = h_ref.shape[0]
     total = mine_ref[...] + other_ref[...]
     sigma = (total + total.T) * weight_ref[...]
     diagonal = eye(norb)
-    inverse_row = 1.0 / onsite_ref[...]
+    row = levels_ref[place[0]]
+    inverse_row = 1.0 / row[:, :norb]
     inverse_column = jnp.broadcast_to(inverse_row, (8, norb)).T[:, :1]
     (s,) = series([(h_ref[...] + sigma) * inverse_row])
     green = split(jnp.where(diagonal, 1.0 + s, s) * inverse_column)
-    source = jnp.where(diagonal, sigma + inject_ref[...], sigma)
+    source = jnp.where(diagonal, sigma + row[:, norb:], sigma)
     lesser = dot3(split(dot3(green, split(source))), green, ((1,), (1,)))
     return lesser, jnp.sum(jnp.where(diagonal, lesser, 0.0), axis=0, keepdims=True)
 
 
 def second_kernel(
-    listed_t, lanes_ref, weight_ref, mine_ref, other_ref, h_ref, onsite_ref, inject_ref,
+    place, listed_t, lanes_ref, weight_ref, mine_ref, other_ref, h_ref, levels_ref,
     out_ref, density_ref, lesser_ref,
 ):
     lesser, density_ref[...] = lesser_function(
-        weight_ref, mine_ref, other_ref, h_ref, onsite_ref, inject_ref
+        place, weight_ref, mine_ref, other_ref, h_ref, levels_ref
     )
     lesser_ref[...] = lesser
     norb = lesser_ref.shape[0]
@@ -195,7 +233,8 @@
         out_ref[pl.ds(k, count, stride=stride), :] = parts[k]
 
 
-def last_kernel(coupling_ref, in_ref, out_ref):
+def last_kernel(coupling_ref, in_ref, diagonal_ref, out_ref, density_ref):
+    density_ref[...] = diagonal_ref[...]
     listed, tiles, size = out_ref.shape
     parts = size // LANES
     for j in range(listed):
@@ -206,11 +245,11 @@
 
 
 def row_kernel(
-    listed_t, weight_ref, mine_ref, other_ref, h_ref, onsite_ref, inject_ref,
+    place, listed_t, weight_ref, mine_ref, other_ref, h_ref, levels_ref,
     out_ref, density_ref, lesser_ref, flat,
 ):
     lesser, density_ref[...] = lesser_function(
-        weight_ref, mine_ref, other_ref, h_ref, onsite_ref, inject_ref
+        place, weight_ref, mine_ref, other_ref, h_ref, levels_ref
     )
     lesser_ref[...] = lesser
     norb = lesser_ref.shape[0]
@@ -256,7 +295,8 @@
         out_ref[:, :, part] = mixed.reshape(count, 1, LANES)
 
 
-def row_last_kernel(coupling, in_ref, out_ref):
+def row_last_kernel(coupling, in_ref, diagonal_ref, out_ref, density_ref):
+    density_ref[...] = diagonal_ref[...]
     listed, tiles, size = out_ref.shape
     per = in_ref.shape[2] // LANES
     for t in range(tiles):
@@ -282,52 +322,66 @@
     def exchange(x):
         return lax.all_to_all(x, axes, split_axis=0, concat_axis=0, tiled=True)
 
-    levels = call(levels_kernel, array(count, 1, 2 * norb), [VMEM] * 2)(onsite, inject)
-    levels = exchange(levels)
-    weight, lanes = call(
-        tables_kernel,
-        (array(norb, norb), array(tiles, LANES, dtype=jnp.int32)),
-        [SMEM] * 2,
-    )(listed_t, coupling)
-
+    levels = call(
+        levels_kernel,
+        array(count, 1, 2 * norb),
+        [HBM] * 2,
+        [pltpu.VMEM((2, 1, norb), f32), pltpu.SemaphoreType.DMA((2,))],
+        vmem=60,
+    )(onsite, inject)
+    all_levels = exchange(levels)
     me = lax.axis_index("energy") * tile_count + lax.axis_index("tile")
+    place = jnp.reshape(me, (1,)).astype(jnp.int32)
     half = count // 2
+    energy_flops = 14 * 2 * norb**3
+    dense = array(norb, norb)
+    weight, lanes, mine, other = call(
+        own_kernel,
+        (dense, array(tiles, LANES, dtype=jnp.int32), dense, dense),
+        [SMEM] * 4 + [VMEM] * 2,
+        flops=energy_flops,
+    )(place, listed_t, coupling, phonon_kernel, hamiltonian, levels)
     mine, other = call(
         first_kernel,
-        (array(norb, norb),) * 2,
-        [SMEM, SMEM, VMEM, VMEM],
-        [pltpu.VMEM((half // UNROLL, norb, LANES), f32)],
+        (dense, dense),
+        [SMEM] * 2 + [VMEM] * 4,
+        [pltpu.VMEM((-(-(half - 1) // UNROLL), norb, LANES), f32)],
         vmem=24,
-        flops=half * 14 * 2 * norb**3,
-    )(jnp.reshape(me, (1,)).astype(jnp.int32), phonon_kernel, levels, hamiltonian)
+        flops=(half - 1) * energy_flops,
+    )(place, phonon_kernel, all_levels, hamiltonian, mine, other)
     other = lax.ppermute(other, "tile", [(i, i + 1 - 2 * (i % 2)) for i in range(tile_count)])
 
-    operands = (weight, mine, other, hamiltonian, onsite, inject)
+    operands = (weight, mine, other, hamiltonian, all_levels)
     green_flops = 18 * 2 * norb**3
-    dense = pltpu.VMEM((norb, norb), f32)
+    scratch = pltpu.VMEM((norb, norb), f32)
+    results = (array(listed, tiles, b * b), array(1, norb))
     if count * LANES == norb * b and listed * b == LANES + b:
         rows = array(norb * listed * b // LANES, LANES)
         pieces, density = call(
-            second_kernel, (rows, array(1, norb)), [SMEM] + [VMEM] * 7, [dense], flops=green_flops
-        )(listed_t, lanes, *operands)
+            second_kernel,
+            (rows, array(1, norb)),
+            [SMEM] * 2 + [VMEM] * 6,
+            [scratch],
+            flops=green_flops,
+        )(place, listed_t, lanes, *operands)
         flat = (count, 1, rows.shape[0] * LANES // count)
         pieces = exchange(pieces.reshape(flat)).reshape(rows.shape)
         pieces = call(mix_kernel, rows, [VMEM] * 2)(phonon_kernel, pieces)
         pieces = exchange(pieces.reshape(flat)).reshape(rows.shape)
-        blocks = call(last_kernel, array(listed, tiles, b * b), [VMEM] * 2)(coupling, pieces)
+        blocks, density = call(last_kernel, results, [VMEM] * 3)(coupling, pieces, density)
     else:
         per = -(-norb * listed * b // (LANES * count))
         rows = array(count, 1, per * LANES)
         pieces, density = call(
             row_kernel,
             (rows, array(1, norb)),
-            [SMEM] + [VMEM] * 6,
-            [dense, pltpu.VMEM((norb // LANES, norb, 1, LANES), f32)],
+            [SMEM] * 2 + [VMEM] * 5,
+            [scratch, pltpu.VMEM((norb // LANES, norb, 1, LANES), f32)],
             flops=green_flops,
-        )(listed_t, *operands)
+        )(place, listed_t, *operands)
         pieces = call(row_mix_kernel, rows, [VMEM] * 2)(phonon_kernel, exchange(pieces))
-        blocks = call(row_last_kernel, array(listed, tiles, b * b), [SMEM, VMEM])(
-            coupling, exchange(pieces)
+        blocks, density = call(row_last_kernel, results, [SMEM, VMEM, VMEM])(
+            coupling, exchange(pieces), density
         )
     return blocks.transpose(1, 0, 2)[None], density
 

time: 55.8 us -> 52.4 us (0.939)
  waiting for transfers between devices: 7.94 us -> 4.93 us
  local copies, waits for them, and re-layouts: 3 us -> 1.65 us
  blocking collectives: 20.3 us -> 20.9 us
    all_to_all x1, waiting for transfers between devices: 7.39 us -> 3.5 us  [exchange(): return lax.all_to_all(x, axes, split_axis=0, concat_axis=0, tiled=True)]
    unnamed x16 -> x12, local copies, waits for them, and re-layouts: 3 us -> 1.65 us
    ppermute x1, waiting for transfers between devices: 0.55 us -> 1.43 us  [local(): lax.ppermute(other, 'tile', [(i, i + 1 - 2 * (i % 2)) for i in range(tile...]
    all_to_all x2, blocking collectives: 20.3 us -> 20.9 us  [exchange(): return lax.all_to_all(x, axes, split_axis=0, concat_axis=0, tiled=True)]
  transfers between devices with their start and end apart: 2 -> 2, of which waited for: 2 -> 2; matrix products, arithmetic and copies ran while one was open for 0% -> 0% of each run, Pallas kernels for 2% -> 4%
where the time goes in v3:
time: 52.4 us; the launch traced here: 52 us
  blocking collectives  20.9 us (40%)
  Pallas kernels  16.3 us (31%)
  starting transfers between devices  7.5 us (14%)
  waiting for transfers between devices  4.93 us (9%)
  local copies, waits for them, and re-layouts  1.65 us (3%)
  between operations  0.74 us (1%)
    all_to_all x2, blocking collectives, exchange(): return lax.all_to_all(x, axes, split_axis=0, concat_axis=0, tiled=True)  20.9 us
    pallas_call x1, Pallas kernels, local(): call(first_kernel, (dense, dense), [SMEM] * 2 + [VMEM] * 4, [pltpu.VMEM((...  9.21 us
    all_to_all x1, starting transfers between devices, exchange(): return lax.all_to_all(x, axes, split_axis=0, concat_axis=0, tiled=True)  7.33 us
    all_to_all x1, waiting for transfers between devices, exchange(): return lax.all_to_all(x, axes, split_axis=0, concat_axis=0, tiled=True)  3.5 us
    pallas_call x1, Pallas kernels, local(): call(second_kernel, (rows, array(1, norb)), [SMEM] * 2 + [VMEM] * 6, [scr...  2.36 us
    pallas_call x1, Pallas kernels, local(): call(own_kernel, (dense, array(tiles, LANES, dtype=jnp.int32), dense, den...  2.23 us
    unnamed x12, local copies, waits for them, and re-layouts  1.65 us
    ppermute x1, waiting for transfers between devices, local(): lax.ppermute(other, 'tile', [(i, i + 1 - 2 * (i % 2)) for i in range(tile...  1.43 us
  transfers between devices with their start and end apart: 2, of which 2 were waited for; matrix products, arithmetic and copies ran while one was open for 0% of the time, Pallas kernels for 4%

profile of v3, /device:TPU:0, one launch (start us, length us, event | category | flops | bytes accessed | tf_op | source)
XLA Modules:
  0.0 52.0 jit_solution(5584190911780377147)
XLA Ops:
  0.6 1.3 %shard_map.77.levels_ref = f32[32,1,512]{2,1,0:T(1,128)} custom-call(f32[1,256]{1,0:T(1,128)} %onsite_ref.1, f32[1,256]{1,0:T(1,128)} %inject_ref.1), custom_call_target="tpu_custom_call" | custom-call | bytes 262144 | tf_op jit(solution)/shard_map/pallas_call | solution.py:325
  2.0 0.0 copy-start
  2.0 0.0 copy-start.2
  2.0 0.0 copy-start.5
  2.0 7.3 %all-to-all-start = ((f32[32,1,512]{2,1,0:T(1,128)}), f32[32,1,512]{2,1,0:T(1,128)S(1)}, u32[]{:S(2)}, u32[]{:S(2)}) async-start(f32[32,1,512]{2,1,0:T(1,128)} %shard_map.77.levels_ref), calls=%async_computation | async-start | bytes 131072 | tf_op jit(solution)/shard_map/all_to_all | solution.py:323
  9.4 0.0 copy-start.1
  9.4 0.0 copy-done
  9.4 0.0 copy-done.2
  9.4 0.0 copy-done.5
  9.4 0.7 %copy-done.1 = f32[32,32]{1,0:T(8,128)S(1)} copy-done((f32[32,32]{1,0:T(8,128)S(1)}, f32[32,32]{1,0:T(8,128)}, u32[]{:S(2)}) %copy-start.1) | copy-done | bytes 4120
  10.1 0.0 copy-start.3
  10.1 0.9 %copy-done.3 = f32[256,256]{1,0:T(8,128)S(1)} copy-done((f32[256,256]{1,0:T(8,128)S(1)}, f32[256,256]{1,0:T(8,128)}, u32[]{:S(2)}) %copy-start.3) | copy-done | bytes 262168
  11.0 0.0 copy-start.4
  11.0 2.2 %shard_map.78 = (f32[256,256]{1,0:T(8,128)S(1)}, s32[16,128]{1,0:T(8,128)S(1)}, f32[256,256]{1,0:T(8,128)S(1)}, f32[256,256]{1,0:T(8,128)S(1)}) custom-call(s32[1]{0:T(128)} %bitcast.place, s32[8,16]{1,0:T(8,128)S(1)} %bitcast.13, f32[16,9]{1,0:T(8,128)S(1)} %copy-done.2, f32[32,32]{1,0:T(8,128)S(1)} %copy-done.1, f32[256,256]{1,0:T(8,128)S(1)} %copy-done.3, ...), custom_call_target="tpu_custom_call" | custom-call | flops 469762048 | bytes 262144 | tf_op jit(solution)/shard_map/pallas_call | solution.py:338
  13.3 3.5 %all-to-all-done.levels_ref = f32[32,1,512]{2,1,0:T(1,128)S(1)} async-done(((f32[32,1,512]{2,1,0:T(1,128)}), f32[32,1,512]{2,1,0:T(1,128)S(1)}, u32[]{:S(2)}, u32[]{:S(2)}) %all-to-all-start) | async-done | bytes 65568 | tf_op jit(solution)/shard_map/all_to_all | solution.py:323
  16.8 0.0 copy-done.4
  16.8 9.2 %shard_map.79 = (f32[256,256]{1,0:T(8,128)S(1)}, f32[256,256]{1,0:T(8,128)S(1)}) custom-call(s32[1]{0:T(128)} %bitcast.place, f32[32,32]{1,0:T(8,128)S(1)} %copy-done.1, f32[32,1,512]{2,1,0:T(1,128)S(1)} %all-to-all-done.levels_ref, f32[256,256]{1,0:T(8,128)S(1)} %copy-done.4, f32[256,256]{1,0:T(8,128)S(1)} %get-tuple-element.14.own_mine_ref, ...), custom_call_target="tpu_custom_call" | custom-call | flops 7046430720 | bytes 262144 | tf_op jit(solution)/shard_map/pallas_call | solution.py:344
  26.0 0.2 collective-permute-start
  26.2 1.4 %collective-permute-done.other_ref = f32[256,256]{1,0:T(8,128)S(1)} collective-permute-done((f32[256,256]{1,0:T(8,128)S(1)}, f32[256,256]{1,0:T(8,128)S(1)}, u32[]{:S(2)}, u32[]{:S(2)}) %collective-permute-start) | collective-permute-done | bytes 262176 | tf_op jit(solution)/shard_map/ppermute | solution.py:352
  27.6 2.4 %shard_map.80 = (f32[288,128]{1,0:T(8,128)S(1)}, f32[1,256]{1,0:T(1,128)S(1)}) custom-call(s32[1]{0:T(128)} %bitcast.place, s32[8,16]{1,0:T(8,128)S(1)} %bitcast.14, s32[16,128]{1,0:T(8,128)S(1)} %get-tuple-element.12.lanes_ref, f32[256,256]{1,0:T(8,128)S(1)} %get-tuple-element.13.weight_ref, f32[256,256]{1,0:T(8,128)S(1)} %get-tuple-element.16.mine_ref, ...), custom_call_target="tpu_custom_call" | custom-call | flops 603979776 | bytes 262144 | tf_op jit(solution)/shard_map/pallas_call | solution.py:360
  30.0 10.6 %all_to_all.15 = f32[32,1,1152]{2,1,0:T(1,128)S(1)} all-to-all(f32[32,1,1152]{2,1,0:T(1,128)S(1)} %bitcast.12), channel_id=1, replica_groups=mesh['energy'=8,'tile'=4] {'energy','tile'}, dimensions={0} | all-to-all | bytes 294912 | tf_op jit(solution)/shard_map/all_to_all | solution.py:323
  40.5 0.4 shard_map.81
  41.0 10.3 %all_to_all.16 = f32[32,1,1152]{2,1,0:T(1,128)S(1)} all-to-all(f32[32,1,1152]{2,1,0:T(1,128)S(1)} %bitcast.11), channel_id=1, replica_groups=mesh['energy'=8,'tile'=4] {'energy','tile'}, dimensions={0} | all-to-all | bytes 294912 | tf_op jit(solution)/shard_map/all_to_all | solution.py:323
  51.3 0.8 %shard_map.82 = (f32[9,16,256]{2,1,0:T(8,128)}, f32[1,256]{1,0:T(1,128)}) custom-call(f32[16,9]{1,0:T(8,128)S(1)} %copy-done.2, f32[288,128]{1,0:T(8,128)S(1)} %bitcast.9, f32[1,256]{1,0:T(1,128)S(1)} %get-tuple-element.19.diagonal_ref), custom_call_target="tpu_custom_call" | custom-call | bytes 262144 | tf_op jit(solution)/shard_map/pallas_call | solution.py:371
Async XLA Ops:
  2.0 7.4 %copy-start = (f32[32,1,512]{2,1,0:T(1,128)S(1)}, f32[32,1,512]{2,1,0:T(1,128)}, u32[]{:S(2)}) copy-start(f32[32,1,512]{2,1,0:T(1,128)} %shard_map.77.levels_ref) | copy-start | bytes 196612
  2.0 7.4 %copy-start.2 = (f32[16,9]{1,0:T(8,128)S(1)}, f32[16,9]{1,0:T(8,128)}, u32[]{:S(2)}) copy-start(f32[16,9]{1,0:T(8,128)} %coupling_ref.1) | copy-start | bytes 1732
  2.0 7.4 %copy-start.5 = (s32[16,8]{0,1:T(8,128)S(1)}, s32[16,8]{0,1:T(8,128)}, u32[]{:S(2)}) copy-start(s32[16,8]{0,1:T(8,128)} %param.11) | copy-start | bytes 1540
  2.0 14.7 %all-to-all-start = ((f32[32,1,512]{2,1,0:T(1,128)}), f32[32,1,512]{2,1,0:T(1,128)S(1)}, u32[]{:S(2)}, u32[]{:S(2)}) async-start(f32[32,1,512]{2,1,0:T(1,128)} %shard_map.77.levels_ref), calls=%async_computation | async-start | bytes 131072 | tf_op jit(solution)/shard_map/all_to_all | solution.py:323
  9.4 0.7 %copy-start.1 = (f32[32,32]{1,0:T(8,128)S(1)}, f32[32,32]{1,0:T(8,128)}, u32[]{:S(2)}) copy-start(f32[32,32]{1,0:T(8,128)} %kernel_ref.5) | copy-start | bytes 12292
  10.1 0.9 %copy-start.3 = (f32[256,256]{1,0:T(8,128)S(1)}, f32[256,256]{1,0:T(8,128)}, u32[]{:S(2)}) copy-start(f32[256,256]{1,0:T(8,128)} %h_ref.5) | copy-start | bytes 786436
  11.0 5.7 %copy-start.4 = (f32[256,256]{1,0:T(8,128)S(1)}, f32[256,256]{1,0:T(8,128)}, u32[]{:S(2)}) copy-start(f32[256,256]{1,0:T(8,128)} %h_ref.5) | copy-start | bytes 786436
  26.0 1.6 %collective-permute-start = (f32[256,256]{1,0:T(8,128)S(1)}, f32[256,256]{1,0:T(8,128)S(1)}, u32[]{:S(2)}, u32[]{:S(2)}) collective-permute-start(f32[256,256]{1,0:T(8,128)S(1)} %get-tuple-element.17), channel_id=1, source_target_pairs={{0,1},{1,0},{2,3},{3,2},{4,5},{5,4},{6,7},{7,6},{8,9},{9,8},{10,11... | collective-permute-start | bytes 786440 | tf_op jit(solution)/shard_map/ppermute | solution.py:352

commit v4 on v3

--- a/solution.py
+++ b/solution.py
@@ -58,6 +58,16 @@
         compiler_params=pltpu.CompilerParams(vmem_limit_bytes=vmem << 20),
         cost_estimate=pl.CostEstimate(flops=flops, bytes_accessed=1 << 18, transcendentals=0),
     )
+
+
+def position():
+    me = lax.axis_index("energy") * lax.axis_size("tile") + lax.axis_index("tile")
+    return me, me + 1 - 2 * lax.rem(me, 2)
+
+
+def energy_of(k, half):
+    me, _ = position()
+    return 2 * lax.rem(me // 2 + jnp.minimum(k, half - 1), half) + lax.rem(me, 2)
 
 
 def levels_kernel(onsite_ref, inject_ref, out_ref, rows, sems):
@@ -90,18 +100,23 @@
 
 
 def own_kernel(
-    place, listed_t, coupling, kernel_ref, h_ref, levels_ref,
-    weight_ref, lanes_ref, mine_ref, other_ref,
+    listed_t, coupling, kernel_ref, h_ref, levels_ref,
+    weight_ref, lanes_ref, row_ref, scales_ref, mine_ref, other_ref,
 ):
     tiles, listed = coupling.shape
     norb = weight_ref.shape[0]
     b = norb // tiles
     row = levels_ref[0]
+    row_ref[...] = row
     column = jnp.broadcast_to(1.0 / row[:, :norb], (8, norb)).T[:, :1]
-    me = place[0]
-    partner = me + 1 - 2 * lax.rem(me, 2)
+    me, partner = position()
     scales = [[kernel_ref[target, me]] for target in (me, partner)]
     mine_ref[...], other_ref[...] = weighted(h_ref, [row], [column], scales)
+    half = kernel_ref.shape[0] // 2
+    for i, target in enumerate((me, partner)):
+        for k in range(1, scales_ref.shape[1]):
+            scale = kernel_ref[target, energy_of(k, half)] if k < half else 0.0
+            scales_ref[i, k] = jnp.full((1, LANES), scale, f32)
     group = lax.broadcasted_iota(jnp.int32, (b, norb), 1) // b
     slot = lax.broadcasted_iota(jnp.int32, (1, LANES), 1) // b
     for t in range(tiles):
@@ -112,39 +127,31 @@
             weight = jnp.where(group == m, coupling[t, j], weight)
             tile = jnp.where(slot == j, m, tile)
         weight_ref[pl.ds(t * b, b), :] = weight
-        lanes_ref[pl.ds(t, 1), :] = tile
+        lanes_ref[pl.ds(t, 1), :LANES] = tile
+        lanes_ref[pl.ds(t, 1), LANES:] = jnp.full((1, LANES), listed_t[listed - 2, t], jnp.int32)
 
 
 def first_kernel(
-    place, kernel_ref, levels_ref, h_ref, own_mine_ref, own_other_ref,
-    mine_ref, other_ref, columns,
+    scales_ref, levels_ref, h_ref, own_mine_ref, own_other_ref, mine_ref, other_ref, columns
 ):
     norb = h_ref.shape[0]
     half = levels_ref.shape[0] // 2
-    me = place[0]
-    parity = lax.rem(me, 2)
-    partner = me + 1 - 2 * parity
     groups = columns.shape[0]
-    unroll = -(-(half - 1) // groups)
-
-    def energy(k):
-        return 2 * lax.rem(me // 2 + jnp.minimum(k, half - 1), half) + parity
-
-    def fill(g):
-        rows = [levels_ref[energy(1 + g * unroll + u % unroll), :, :norb] for u in range(8)]
+    unroll = (scales_ref.shape[1] - 1) // groups
+    for g in range(groups):
+        rows = [
+            levels_ref[energy_of(1 + g * unroll + u % unroll, half), :, :norb] for u in range(8)
+        ]
         columns[g, :, :8] = (1.0 / jnp.concatenate(rows, axis=0)).T
-
-    for g in range(groups):
-        fill(g)
     mine_ref[...] = own_mine_ref[...]
     other_ref[...] = own_other_ref[...]
 
     def group(g, carry):
         ks = [1 + g * unroll + u for u in range(unroll)]
-        rows = [levels_ref[energy(k)] for k in ks]
+        rows = [levels_ref[energy_of(k, half)] for k in ks]
         scales = [
-            [jnp.where(k < half, kernel_ref[target, energy(k)], 0.0) for k in ks]
-            for target in (me, partner)
+            [jnp.concatenate([scales_ref[i, k]] * (norb // LANES), axis=1) for k in ks]
+            for i in range(2)
         ]
         mine, other = weighted(
             h_ref, rows, [columns[g, :, u : u + 1] for u in range(unroll)], scales
@@ -156,12 +163,12 @@
     lax.fori_loop(0, groups, group, 0)
 
 
-def lesser_function(place, weight_ref, mine_ref, other_ref, h_ref, levels_ref):
+def lesser_function(weight_ref, mine_ref, other_ref, h_ref, row_ref):
     norb = h_ref.shape[0]
     total = mine_ref[...] + other_ref[...]
     sigma = (total + total.T) * weight_ref[...]
     diagonal = eye(norb)
-    row = levels_ref[place[0]]
+    row = row_ref[...]
     inverse_row = 1.0 / row[:, :norb]
     inverse_column = jnp.broadcast_to(inverse_row, (8, norb)).T[:, :1]
     (s,) = series([(h_ref[...] + sigma) * inverse_row])
@@ -172,41 +179,40 @@
 
 
 def second_kernel(
-    place, listed_t, lanes_ref, weight_ref, mine_ref, other_ref, h_ref, levels_ref,
+    lanes_ref, weight_ref, mine_ref, other_ref, h_ref, row_ref,
     out_ref, density_ref, lesser_ref,
 ):
     lesser, density_ref[...] = lesser_function(
-        place, weight_ref, mine_ref, other_ref, h_ref, levels_ref
+        weight_ref, mine_ref, other_ref, h_ref, row_ref
     )
     lesser_ref[...] = lesser
     norb = lesser_ref.shape[0]
     tiles = lanes_ref.shape[0]
     b = norb // tiles
-    last = listed_t.shape[0]
     per = LANES // b
     shape = (per, LANES)
     lane = lax.broadcasted_iota(jnp.int32, shape, 1)
     own = lane // b == lax.broadcasted_iota(jnp.int32, shape, 0)
 
-    def take(values, tile):
+    def take(rows, tile):
         index = lax.rem(tile, per) * b + lax.rem(lane, b)
-        return jnp.take_along_axis(values, index, axis=1, mode="promise_in_bounds")
+        value = None
+        for h in range(norb // LANES):
+            part = jnp.take_along_axis(
+                lesser_ref[rows, pl.ds(h * LANES, LANES)], index, axis=1, mode="promise_in_bounds"
+            )
+            value = part if value is None else jnp.where(tile // per == h, part, value)
+        return value
 
     for t in range(tiles):
-        tile = jnp.broadcast_to(lanes_ref[pl.ds(t, 1), :], shape)
-        m = listed_t[last - 1, t]
+        tile = jnp.broadcast_to(lanes_ref[pl.ds(t, 1), :LANES], shape)
+        last = jnp.broadcast_to(lanes_ref[pl.ds(t, 1), LANES:], shape)
         for part in range(b // per):
             rows = pl.ds(t * b + part * per, per)
-            value = take(lesser_ref[rows, :LANES], tile)
-            for h in range(1, norb // LANES):
-                columns = pl.ds(h * LANES, LANES)
-                value = jnp.where(tile // per == h, take(lesser_ref[rows, columns], tile), value)
-            columns = pl.ds(pl.multiple_of(m // per * LANES, LANES), LANES)
-            block = take(lesser_ref[rows, columns], jnp.full(shape, m, jnp.int32))
             first = (t * (b // per) + part) * (per + 1)
-            out_ref[pl.ds(first, per), :] = value
+            out_ref[pl.ds(first, per), :] = take(rows, tile)
             out_ref[pl.ds(first + per, 1), :] = jnp.sum(
-                jnp.where(own, block, 0.0), axis=0, keepdims=True
+                jnp.where(own, take(rows, last), 0.0), axis=0, keepdims=True
             )
 
 
@@ -245,11 +251,11 @@
 
 
 def row_kernel(
-    place, listed_t, weight_ref, mine_ref, other_ref, h_ref, levels_ref,
+    listed_t, weight_ref, mine_ref, other_ref, h_ref, row_ref,
     out_ref, density_ref, lesser_ref, flat,
 ):
     lesser, density_ref[...] = lesser_function(
-        place, weight_ref, mine_ref, other_ref, h_ref, levels_ref
+        weight_ref, mine_ref, other_ref, h_ref, row_ref
     )
     lesser_ref[...] = lesser
     norb = lesser_ref.shape[0]
@@ -330,28 +336,29 @@
         vmem=60,
     )(onsite, inject)
     all_levels = exchange(levels)
-    me = lax.axis_index("energy") * tile_count + lax.axis_index("tile")
-    place = jnp.reshape(me, (1,)).astype(jnp.int32)
     half = count // 2
+    groups = -(-(half - 1) // UNROLL)
     energy_flops = 14 * 2 * norb**3
     dense = array(norb, norb)
-    weight, lanes, mine, other = call(
+    scales = array(2, 1 + groups * UNROLL, 1, LANES)
+    lanes = array(tiles, 2 * LANES, dtype=jnp.int32)
+    weight, lanes, row, scales, mine, other = call(
         own_kernel,
-        (dense, array(tiles, LANES, dtype=jnp.int32), dense, dense),
-        [SMEM] * 4 + [VMEM] * 2,
+        (dense, lanes, array(1, 2 * norb), scales, dense, dense),
+        [SMEM] * 3 + [VMEM] * 2,
         flops=energy_flops,
-    )(place, listed_t, coupling, phonon_kernel, hamiltonian, levels)
+    )(listed_t, coupling, phonon_kernel, hamiltonian, levels)
     mine, other = call(
         first_kernel,
         (dense, dense),
-        [SMEM] * 2 + [VMEM] * 4,
-        [pltpu.VMEM((-(-(half - 1) // UNROLL), norb, LANES), f32)],
+        [VMEM] * 5,
+        [pltpu.VMEM((groups, norb, LANES), f32)],
         vmem=24,
         flops=(half - 1) * energy_flops,
-    )(place, phonon_kernel, all_levels, hamiltonian, mine, other)
+    )(scales, all_levels, hamiltonian, mine, other)
     other = lax.ppermute(other, "tile", [(i, i + 1 - 2 * (i % 2)) for i in range(tile_count)])
 
-    operands = (weight, mine, other, hamiltonian, all_levels)
+    operands = (weight, mine, other, hamiltonian, row)
     green_flops = 18 * 2 * norb**3
     scratch = pltpu.VMEM((norb, norb), f32)
     results = (array(listed, tiles, b * b), array(1, norb))
@@ -360,10 +367,10 @@
         pieces, density = call(
             second_kernel,
             (rows, array(1, norb)),
-            [SMEM] * 2 + [VMEM] * 6,
+            [VMEM] * 6,
             [scratch],
             flops=green_flops,
-        )(place, listed_t, lanes, *operands)
+        )(lanes, *operands)
         flat = (count, 1, rows.shape[0] * LANES // count)
         pieces = exchange(pieces.reshape(flat)).reshape(rows.shape)
         pieces = call(mix_kernel, rows, [VMEM] * 2)(phonon_kernel, pieces)
@@ -375,10 +382,10 @@
         pieces, density = call(
             row_kernel,
             (rows, array(1, norb)),
-            [SMEM] * 2 + [VMEM] * 5,
+            [SMEM] + [VMEM] * 5,
             [scratch, pltpu.VMEM((norb // LANES, norb, 1, LANES), f32)],
             flops=green_flops,
-        )(place, listed_t, *operands)
+        )(listed_t, *operands)
         pieces = call(row_mix_kernel, rows, [VMEM] * 2)(phonon_kernel, exchange(pieces))
         blocks, density = call(row_last_kernel, results, [SMEM, VMEM, VMEM])(
             coupling, exchange(pieces), density

time: 52.4 us -> 50.5 us (0.964)
  Pallas kernels: 16.3 us -> 15.1 us
  local copies, waits for them, and re-layouts: 1.65 us -> 0.97 us
  waiting for transfers between devices: 4.93 us -> 5.53 us
  blocking collectives: 20.9 us -> 20.3 us
    pallas_call x3, Pallas kernels: 13.8 us -> 12.5 us  [the longest x1 8.39 us: local(): call(first_kernel, (dense, dense), [VMEM] * 5, [pltpu.VMEM((groups, norb,...]
    unnamed x12, local copies, waits for them, and re-layouts: 1.65 us -> 0.97 us
    all_to_all x1, waiting for transfers between devices: 3.5 us -> 4.12 us  [exchange(): return lax.all_to_all(x, axes, split_axis=0, concat_axis=0, tiled=True)]
    all_to_all x2, blocking collectives: 20.9 us -> 20.3 us  [exchange(): return lax.all_to_all(x, axes, split_axis=0, concat_axis=0, tiled=True)]
  transfers between devices with their start and end apart: 2 -> 2, of which waited for: 2 -> 2; matrix products, arithmetic and copies ran while one was open for 0% -> 0% of each run, Pallas kernels for 4% -> 5%
where the time goes in v4:
time: 50.5 us; the launch traced here: 50.2 us
  blocking collectives  20.3 us (40%)
  Pallas kernels  15.1 us (30%)
  starting transfers between devices  7.52 us (15%)
  waiting for transfers between devices  5.53 us (11%)
  local copies, waits for them, and re-layouts  0.97 us (2%)
  between operations  0.75 us (1%)
    all_to_all x2, blocking collectives, exchange(): return lax.all_to_all(x, axes, split_axis=0, concat_axis=0, tiled=True)  20.3 us
    pallas_call x1, Pallas kernels, local(): call(first_kernel, (dense, dense), [VMEM] * 5, [pltpu.VMEM((groups, norb,...  8.39 us
    all_to_all x1, starting transfers between devices, exchange(): return lax.all_to_all(x, axes, split_axis=0, concat_axis=0, tiled=True)  7.33 us
    all_to_all x1, waiting for transfers between devices, exchange(): return lax.all_to_all(x, axes, split_axis=0, concat_axis=0, tiled=True)  4.12 us
    pallas_call x1, Pallas kernels, local(): call(own_kernel, (dense, lanes, array(1, 2 * norb), scales, dense, dense)...  2.29 us
    pallas_call x1, Pallas kernels, local(): call(second_kernel, (rows, array(1, norb)), [VMEM] * 6, [scratch], flops=...  1.87 us
    ppermute x1, waiting for transfers between devices, local(): lax.ppermute(other, 'tile', [(i, i + 1 - 2 * (i % 2)) for i in range(tile...  1.41 us
    pallas_call x1, Pallas kernels, local(): call(levels_kernel, array(count, 1, 2 * norb), [HBM] * 2, [pltpu.VMEM((2,...  1.35 us
  transfers between devices with their start and end apart: 2, of which 2 were waited for; matrix products, arithmetic and copies ran while one was open for 0% of the time, Pallas kernels for 5%

profile of v4, /device:TPU:0, one launch (start us, length us, event | category | flops | bytes accessed | tf_op | source)
XLA Modules:
  0.0 50.2 jit_solution(2094903973908746358)
XLA Ops:
  0.6 1.3 %shard_map.77.levels_ref = f32[32,1,512]{2,1,0:T(1,128)} custom-call(f32[1,256]{1,0:T(1,128)} %onsite_ref.1, f32[1,256]{1,0:T(1,128)} %inject_ref.1), custom_call_target="tpu_custom_call" | custom-call | bytes 262144 | tf_op jit(solution)/shard_map/pallas_call | solution.py:331
  2.0 0.0 copy-start
  2.0 0.0 copy-start.1
  2.0 0.0 copy-start.2
  2.0 0.0 copy-start.5
  2.0 7.3 %all-to-all-start = ((f32[32,1,512]{2,1,0:T(1,128)}), f32[32,1,512]{2,1,0:T(1,128)S(1)}, u32[]{:S(2)}, u32[]{:S(2)}) async-start(f32[32,1,512]{2,1,0:T(1,128)} %shard_map.77.levels_ref), calls=%async_computation | async-start | bytes 131072 | tf_op jit(solution)/shard_map/all_to_all | solution.py:329
  9.4 0.0 copy-done
  9.4 0.0 copy-done.1
  9.4 0.0 copy-done.2
  9.4 0.0 copy-done.5
  9.4 0.0 copy-start.3
  9.4 0.9 %copy-done.3 = f32[256,256]{1,0:T(8,128)S(1)} copy-done((f32[256,256]{1,0:T(8,128)S(1)}, f32[256,256]{1,0:T(8,128)}, u32[]{:S(2)}) %copy-start.3) | copy-done | bytes 262168
  10.4 0.0 copy-start.4
  10.4 2.3 %shard_map.78 = (f32[256,256]{1,0:T(8,128)S(1)}, s32[16,256]{1,0:T(8,128)S(1)}, f32[1,512]{1,0:T(1,128)S(1)}, f32[2,16,1,128]{3,2,1,0:T(1,128)S(1)}, f32[256,256]{1,0:T(8,128)S(1)}, /*index=5*/f32[256,256]{1,0:T(8,128)S(1)}) custom-call(s32[8,16]{1,0:T(8,128)S(1)} %bitcast.12, f32[16,9]{1,0:T(8,128)S(1)} %copy-done.2, f32[32,32]{1,0:T(8,128)S(1)} %copy-done.1, ...), custom_call_target="tpu_custom_call" | custom-call | flops 469762048 | bytes 262144 | tf_op jit(solution)/shard_map/pallas_call | solution.py:345
  12.7 4.1 %all-to-all-done.levels_ref = f32[32,1,512]{2,1,0:T(1,128)S(1)} async-done(((f32[32,1,512]{2,1,0:T(1,128)}), f32[32,1,512]{2,1,0:T(1,128)S(1)}, u32[]{:S(2)}, u32[]{:S(2)}) %all-to-all-start) | async-done | bytes 65568 | tf_op jit(solution)/shard_map/all_to_all | solution.py:329
  16.8 0.0 copy-done.4
  16.8 8.4 %shard_map.79 = (f32[256,256]{1,0:T(8,128)S(1)}, f32[256,256]{1,0:T(8,128)S(1)}) custom-call(f32[2,16,1,128]{3,2,1,0:T(1,128)S(1)} %get-tuple-element.16.scales_ref, f32[32,1,512]{2,1,0:T(1,128)S(1)} %all-to-all-done.levels_ref, f32[256,256]{1,0:T(8,128)S(1)} %copy-done.4, f32[256,256]{1,0:T(8,128)S(1)} %get-tuple-element.17.own_mine_ref, ...), custom_call_target="tpu_custom_call" | custom-call | flops 7046430720 | bytes 262144 | tf_op jit(solution)/shard_map/pallas_call | solution.py:351
  25.2 0.2 collective-permute-start
  25.4 1.4 %collective-permute-done.other_ref = f32[256,256]{1,0:T(8,128)S(1)} collective-permute-done((f32[256,256]{1,0:T(8,128)S(1)}, f32[256,256]{1,0:T(8,128)S(1)}, u32[]{:S(2)}, u32[]{:S(2)}) %collective-permute-start) | collective-permute-done | bytes 262176 | tf_op jit(solution)/shard_map/ppermute | solution.py:359
  26.8 1.9 %shard_map.80 = (f32[288,128]{1,0:T(8,128)S(1)}, f32[1,256]{1,0:T(1,128)S(1)}) custom-call(s32[16,256]{1,0:T(8,128)S(1)} %get-tuple-element.14.lanes_ref, f32[256,256]{1,0:T(8,128)S(1)} %get-tuple-element.15.weight_ref, f32[256,256]{1,0:T(8,128)S(1)} %get-tuple-element.19.mine_ref, f32[256,256]{1,0:T(8,128)S(1)} %collective-permute-done.other_ref, ...), custom_call_target="tpu_custom_call" | custom-call | flops 603979776 | bytes 262144 | tf_op jit(solution)/shard_map/pallas_call | solution.py:367
  28.7 10.1 %all_to_all.15 = f32[32,1,1152]{2,1,0:T(1,128)S(1)} all-to-all(f32[32,1,1152]{2,1,0:T(1,128)S(1)} %bitcast.11), channel_id=1, replica_groups=mesh['energy'=8,'tile'=4] {'energy','tile'}, dimensions={0} | all-to-all | bytes 294912 | tf_op jit(solution)/shard_map/all_to_all | solution.py:329
  38.8 0.4 shard_map.81
  39.2 10.2 %all_to_all.16 = f32[32,1,1152]{2,1,0:T(1,128)S(1)} all-to-all(f32[32,1,1152]{2,1,0:T(1,128)S(1)} %bitcast.10), channel_id=1, replica_groups=mesh['energy'=8,'tile'=4] {'energy','tile'}, dimensions={0} | all-to-all | bytes 294912 | tf_op jit(solution)/shard_map/all_to_all | solution.py:329
  49.5 0.8 %shard_map.82 = (f32[9,16,256]{2,1,0:T(8,128)}, f32[1,256]{1,0:T(1,128)}) custom-call(f32[16,9]{1,0:T(8,128)S(1)} %copy-done.2, f32[288,128]{1,0:T(8,128)S(1)} %bitcast.8, f32[1,256]{1,0:T(1,128)S(1)} %get-tuple-element.23.diagonal_ref), custom_call_target="tpu_custom_call" | custom-call | bytes 262144 | tf_op jit(solution)/shard_map/pallas_call | solution.py:378
Async XLA Ops:
  2.0 7.4 %copy-start = (f32[32,1,512]{2,1,0:T(1,128)S(1)}, f32[32,1,512]{2,1,0:T(1,128)}, u32[]{:S(2)}) copy-start(f32[32,1,512]{2,1,0:T(1,128)} %shard_map.77.levels_ref) | copy-start | bytes 196612
  2.0 7.4 %copy-start.1 = (f32[32,32]{1,0:T(8,128)S(1)}, f32[32,32]{1,0:T(8,128)}, u32[]{:S(2)}) copy-start(f32[32,32]{1,0:T(8,128)} %kernel_ref.3) | copy-start | bytes 12292
  2.0 7.4 %copy-start.2 = (f32[16,9]{1,0:T(8,128)S(1)}, f32[16,9]{1,0:T(8,128)}, u32[]{:S(2)}) copy-start(f32[16,9]{1,0:T(8,128)} %coupling_ref.1) | copy-start | bytes 1732
  2.0 7.4 %copy-start.5 = (s32[16,8]{0,1:T(8,128)S(1)}, s32[16,8]{0,1:T(8,128)}, u32[]{:S(2)}) copy-start(s32[16,8]{0,1:T(8,128)} %param.11) | copy-start | bytes 1540
  2.0 14.7 %all-to-all-start = ((f32[32,1,512]{2,1,0:T(1,128)}), f32[32,1,512]{2,1,0:T(1,128)S(1)}, u32[]{:S(2)}, u32[]{:S(2)}) async-start(f32[32,1,512]{2,1,0:T(1,128)} %shard_map.77.levels_ref), calls=%async_computation | async-start | bytes 131072 | tf_op jit(solution)/shard_map/all_to_all | solution.py:329
  9.4 1.0 %copy-start.3 = (f32[256,256]{1,0:T(8,128)S(1)}, f32[256,256]{1,0:T(8,128)}, u32[]{:S(2)}) copy-start(f32[256,256]{1,0:T(8,128)} %h_ref.5) | copy-start | bytes 786436
  10.4 6.4 %copy-start.4 = (f32[256,256]{1,0:T(8,128)S(1)}, f32[256,256]{1,0:T(8,128)}, u32[]{:S(2)}) copy-start(f32[256,256]{1,0:T(8,128)} %h_ref.5) | copy-start | bytes 786436
  25.2 1.6 %collective-permute-start = (f32[256,256]{1,0:T(8,128)S(1)}, f32[256,256]{1,0:T(8,128)S(1)}, u32[]{:S(2)}, u32[]{:S(2)}) collective-permute-start(f32[256,256]{1,0:T(8,128)S(1)} %get-tuple-element.20), channel_id=1, source_target_pairs={{0,1},{1,0},{2,3},{3,2},{4,5},{5,4},{6,7},{7,6},{8,9},{9,8},{10,11... | collective-permute-start | bytes 786440 | tf_op jit(solution)/shard_map/ppermute | solution.py:359

commit v5 on v4

--- a/solution.py
+++ b/solution.py
@@ -11,7 +11,6 @@
 f32 = jnp.float32
 VMEM = pl.BlockSpec(memory_space=pltpu.VMEM)
 SMEM = pl.BlockSpec(memory_space=pltpu.SMEM)
-HBM = pl.BlockSpec(memory_space=pltpu.HBM)
 
 
 def split(x):
@@ -70,28 +69,14 @@
     return 2 * lax.rem(me // 2 + jnp.minimum(k, half - 1), half) + lax.rem(me, 2)
 
 
-def levels_kernel(onsite_ref, inject_ref, out_ref, rows, sems):
-    count, _, width = out_ref.shape
-    norb = width // 2
-    copies = [
-        pltpu.make_async_copy(ref, rows.at[i], sems.at[i])
-        for i, ref in enumerate((onsite_ref, inject_ref))
-    ]
-    for copy in copies:
-        copy.start()
-    for i, copy in enumerate(copies):
-        copy.wait()
-        out_ref[:, :, pl.ds(i * norb, norb)] = jnp.broadcast_to(rows[i][None], (count, 1, norb))
-
-
 def weighted(h_ref, rows, columns, scales):
     norb = h_ref.shape[0]
     diagonal = eye(norb)
-    sums = series([h_ref[...] * (1.0 / row[:, :norb]) for row in rows])
+    sums = series([h_ref[...] * (1.0 / row[:1]) for row in rows])
     totals = [None] * len(scales)
     for u, row in enumerate(rows):
         root = jnp.where(diagonal, 1.0 + sums[u], sums[u]) * columns[u]
-        high, low = split(root * jnp.sqrt(row[:, norb:]))
+        high, low = split(root * jnp.sqrt(row[1:]))
         flip = ((1,), (1,))
         part = dot(high, high * jnp.bfloat16(0.5), flip) + dot(high, low, flip)
         for i, scale in enumerate(scales):
@@ -100,15 +85,14 @@
 
 
 def own_kernel(
-    listed_t, coupling, kernel_ref, h_ref, levels_ref,
-    weight_ref, lanes_ref, row_ref, scales_ref, mine_ref, other_ref,
+    listed_t, coupling, kernel_ref, h_ref, row_ref,
+    weight_ref, lanes_ref, scales_ref, mine_ref, other_ref,
 ):
     tiles, listed = coupling.shape
     norb = weight_ref.shape[0]
     b = norb // tiles
-    row = levels_ref[0]
-    row_ref[...] = row
-    column = jnp.broadcast_to(1.0 / row[:, :norb], (8, norb)).T[:, :1]
+    row = row_ref[...]
+    column = jnp.broadcast_to(1.0 / row[:1], (8, norb)).T[:, :1]
     me, partner = position()
     scales = [[kernel_ref[target, me]] for target in (me, partner)]
     mine_ref[...], other_ref[...] = weighted(h_ref, [row], [column], scales)
@@ -140,7 +124,7 @@
     unroll = (scales_ref.shape[1] - 1) // groups
     for g in range(groups):
         rows = [
-            levels_ref[energy_of(1 + g * unroll + u % unroll, half), :, :norb] for u in range(8)
+            levels_ref[energy_of(1 + g * unroll + u % unroll, half), :1] for u in range(8)
         ]
         columns[g, :, :8] = (1.0 / jnp.concatenate(rows, axis=0)).T
     mine_ref[...] = own_mine_ref[...]
@@ -169,11 +153,11 @@
     sigma = (total + total.T) * weight_ref[...]
     diagonal = eye(norb)
     row = row_ref[...]
-    inverse_row = 1.0 / row[:, :norb]
+    inverse_row = 1.0 / row[:1]
     inverse_column = jnp.broadcast_to(inverse_row, (8, norb)).T[:, :1]
     (s,) = series([(h_ref[...] + sigma) * inverse_row])
     green = split(jnp.where(diagonal, 1.0 + s, s) * inverse_column)
-    source = jnp.where(diagonal, sigma + row[:, norb:], sigma)
+    source = jnp.where(diagonal, sigma + row[1:], sigma)
     lesser = dot3(split(dot3(green, split(source))), green, ((1,), (1,)))
     return lesser, jnp.sum(jnp.where(diagonal, lesser, 0.0), axis=0, keepdims=True)
 
@@ -328,26 +312,20 @@
     def exchange(x):
         return lax.all_to_all(x, axes, split_axis=0, concat_axis=0, tiled=True)
 
-    levels = call(
-        levels_kernel,
-        array(count, 1, 2 * norb),
-        [HBM] * 2,
-        [pltpu.VMEM((2, 1, norb), f32), pltpu.SemaphoreType.DMA((2,))],
-        vmem=60,
-    )(onsite, inject)
-    all_levels = exchange(levels)
+    row = jnp.stack([onsite, inject], axis=1).reshape(2, norb)
+    all_levels = exchange(jnp.broadcast_to(row[None], (count, 2, norb)))
     half = count // 2
     groups = -(-(half - 1) // UNROLL)
     energy_flops = 14 * 2 * norb**3
     dense = array(norb, norb)
     scales = array(2, 1 + groups * UNROLL, 1, LANES)
     lanes = array(tiles, 2 * LANES, dtype=jnp.int32)
-    weight, lanes, row, scales, mine, other = call(
+    weight, lanes, scales, mine, other = call(
         own_kernel,
-        (dense, lanes, array(1, 2 * norb), scales, dense, dense),
+        (dense, lanes, scales, dense, dense),
         [SMEM] * 3 + [VMEM] * 2,
         flops=energy_flops,
-    )(listed_t, coupling, phonon_kernel, hamiltonian, levels)
+    )(listed_t, coupling, phonon_kernel, hamiltonian, row)
     mine, other = call(
         first_kernel,
         (dense, dense),

time: 50.5 us -> 50.5 us (level)
  local copies, waits for them, and re-layouts: 0.97 us -> 2.29 us
  Pallas kernels: 15.1 us -> 13.8 us
    pallas_call x2 -> x1, Pallas kernels: 3.63 us -> 2.29 us  [local(): call(own_kernel, (dense, lanes, scales, dense, dense), [SMEM] * 3 + [VMEM...]
    unnamed x12 -> x14, local copies, waits for them, and re-layouts: 0.97 us -> 1.64 us
    broadcast_in_dim x0 -> x1, local copies, waits for them, and re-layouts: none -> 0.65 us  [local(): all_levels = exchange(jnp.broadcast_to(row[None], (count, 2, norb)))]
where the time goes in v5:
time: 50.5 us; the launch traced here: 50.2 us
  blocking collectives  20.3 us (40%)
  Pallas kernels  13.8 us (27%)
  starting transfers between devices  7.51 us (15%)
  waiting for transfers between devices  5.55 us (11%)
  local copies, waits for them, and re-layouts  2.29 us (5%)
  between operations  0.72 us (1%)
    all_to_all x2, blocking collectives, exchange(): return lax.all_to_all(x, axes, split_axis=0, concat_axis=0, tiled=True)  20.3 us
    pallas_call x1, Pallas kernels, local(): call(first_kernel, (dense, dense), [VMEM] * 5, [pltpu.VMEM((groups, norb,...  8.41 us
    all_to_all x1, starting transfers between devices, exchange(): return lax.all_to_all(x, axes, split_axis=0, concat_axis=0, tiled=True)  7.33 us
    all_to_all x1, waiting for transfers between devices, exchange(): return lax.all_to_all(x, axes, split_axis=0, concat_axis=0, tiled=True)  4.13 us
    pallas_call x1, Pallas kernels, local(): call(own_kernel, (dense, lanes, scales, dense, dense), [SMEM] * 3 + [VMEM...  2.29 us
    pallas_call x1, Pallas kernels, local(): call(second_kernel, (rows, array(1, norb)), [VMEM] * 6, [scratch], flops=...  1.87 us
    unnamed x14, local copies, waits for them, and re-layouts  1.64 us
    ppermute x1, waiting for transfers between devices, local(): lax.ppermute(other, 'tile', [(i, i + 1 - 2 * (i % 2)) for i in range(tile...  1.42 us
  transfers between devices with their start and end apart: 2, of which 2 were waited for; matrix products, arithmetic and copies ran while one was open for 0% of the time, Pallas kernels for 5%

profile of v5, /device:TPU:0, one launch (start us, length us, event | category | flops | bytes accessed | tf_op | source)
XLA Modules:
  0.0 50.2 jit_solution(1350533281053824720)
XLA Ops:
  0.6 0.0 copy-start.6
  0.6 0.0 copy-start.5
  0.6 0.7 %copy-done.6 = f32[1,256]{1,0:T(1,128)S(1)} copy-done((f32[1,256]{1,0:T(1,128)S(1)}, f32[1,256]{1,0:T(1,128)}, u32[]{:S(2)}) %copy-start.6) | copy-done | bytes 1048
  1.3 0.0 copy-done.5
  1.3 0.6 %broadcast_in_dim.8 = f32[32,2,256]{2,1,0:T(2,128)} broadcast(f32[2,256]{1,0:T(2,128)S(1)} %maximum_bitcast_fusion.row_ref), dimensions={1,2} | broadcast | bytes 67584 | tf_op jit(solution)/shard_map/broadcast_in_dim | solution.py:316
  2.0 0.0 copy-start
  2.0 0.0 copy-start.1
  2.0 0.0 copy-start.4
  2.0 7.3 %all-to-all-start = ((f32[32,2,256]{2,1,0:T(2,128)}), f32[32,2,256]{2,1,0:T(2,128)S(1)}, u32[]{:S(2)}, u32[]{:S(2)}) async-start(f32[32,2,256]{2,1,0:T(2,128)} %broadcast_in_dim.8), calls=%async_computation | async-start | bytes 131072 | tf_op jit(solution)/shard_map/all_to_all | solution.py:313
  9.3 0.0 copy-done
  9.3 0.0 copy-done.1
  9.3 0.0 copy-done.4
  9.4 0.0 copy-start.2
  9.4 0.9 %copy-done.2 = f32[256,256]{1,0:T(8,128)S(1)} copy-done((f32[256,256]{1,0:T(8,128)S(1)}, f32[256,256]{1,0:T(8,128)}, u32[]{:S(2)}) %copy-start.2) | copy-done | bytes 262168
  10.3 0.0 copy-start.3
  10.3 2.3 %shard_map.77 = (f32[256,256]{1,0:T(8,128)S(1)}, s32[16,256]{1,0:T(8,128)S(1)}, f32[2,16,1,128]{3,2,1,0:T(1,128)S(1)}, f32[256,256]{1,0:T(8,128)S(1)}, f32[256,256]{1,0:T(8,128)S(1)}) custom-call(s32[8,16]{1,0:T(8,128)S(1)} %bitcast.16, f32[16,9]{1,0:T(8,128)S(1)} %copy-done.1, f32[32,32]{1,0:T(8,128)S(1)} %copy-done, f32[256,256]{1,0:T(8,128)S(1)} %copy-done.2, ...), custom_call_target="tpu_custom_call" | custom-call | flops 469762048 | bytes 262144 | tf_op jit(solution)/shard_map/pallas_call | solution.py:323
  12.6 4.1 %all-to-all-done.levels_ref = f32[32,2,256]{2,1,0:T(2,128)S(1)} async-done(((f32[32,2,256]{2,1,0:T(2,128)}), f32[32,2,256]{2,1,0:T(2,128)S(1)}, u32[]{:S(2)}, u32[]{:S(2)}) %all-to-all-start) | async-done | bytes 65568 | tf_op jit(solution)/shard_map/all_to_all | solution.py:313
  16.7 0.0 copy-done.3
  16.7 8.4 %shard_map.78 = (f32[256,256]{1,0:T(8,128)S(1)}, f32[256,256]{1,0:T(8,128)S(1)}) custom-call(f32[2,16,1,128]{3,2,1,0:T(1,128)S(1)} %get-tuple-element.15.scales_ref, f32[32,2,256]{2,1,0:T(2,128)S(1)} %all-to-all-done.levels_ref, f32[256,256]{1,0:T(8,128)S(1)} %copy-done.3, f32[256,256]{1,0:T(8,128)S(1)} %get-tuple-element.16.own_mine_ref, ...), custom_call_target="tpu_custom_call" | custom-call | flops 7046430720 | bytes 262144 | tf_op jit(solution)/shard_map/pallas_call | solution.py:329
  25.2 0.2 collective-permute-start
  25.3 1.4 %collective-permute-done.other_ref = f32[256,256]{1,0:T(8,128)S(1)} collective-permute-done((f32[256,256]{1,0:T(8,128)S(1)}, f32[256,256]{1,0:T(8,128)S(1)}, u32[]{:S(2)}, u32[]{:S(2)}) %collective-permute-start) | collective-permute-done | bytes 262176 | tf_op jit(solution)/shard_map/ppermute | solution.py:337
  26.8 1.9 %shard_map.79 = (f32[288,128]{1,0:T(8,128)S(1)}, f32[1,256]{1,0:T(1,128)S(1)}) custom-call(s32[16,256]{1,0:T(8,128)S(1)} %get-tuple-element.13.lanes_ref, f32[256,256]{1,0:T(8,128)S(1)} %get-tuple-element.14.weight_ref, f32[256,256]{1,0:T(8,128)S(1)} %get-tuple-element.18.mine_ref, f32[256,256]{1,0:T(8,128)S(1)} %collective-permute-done.other_ref, ...), custom_call_target="tpu_custom_call" | custom-call | flops 603979776 | bytes 262144 | tf_op jit(solution)/shard_map/pallas_call | solution.py:345
  28.6 10.1 %all_to_all.15 = f32[32,1,1152]{2,1,0:T(1,128)S(1)} all-to-all(f32[32,1,1152]{2,1,0:T(1,128)S(1)} %bitcast.15), channel_id=1, replica_groups=mesh['energy'=8,'tile'=4] {'energy','tile'}, dimensions={0} | all-to-all | bytes 294912 | tf_op jit(solution)/shard_map/all_to_all | solution.py:313
  38.7 0.4 shard_map.80
  39.2 10.2 %all_to_all.16 = f32[32,1,1152]{2,1,0:T(1,128)S(1)} all-to-all(f32[32,1,1152]{2,1,0:T(1,128)S(1)} %bitcast.14), channel_id=1, replica_groups=mesh['energy'=8,'tile'=4] {'energy','tile'}, dimensions={0} | all-to-all | bytes 294912 | tf_op jit(solution)/shard_map/all_to_all | solution.py:313
  49.4 0.8 %shard_map.81 = (f32[9,16,256]{2,1,0:T(8,128)}, f32[1,256]{1,0:T(1,128)}) custom-call(f32[16,9]{1,0:T(8,128)S(1)} %copy-done.1, f32[288,128]{1,0:T(8,128)S(1)} %bitcast.12, f32[1,256]{1,0:T(1,128)S(1)} %get-tuple-element.21.diagonal_ref), custom_call_target="tpu_custom_call" | custom-call | bytes 262144 | tf_op jit(solution)/shard_map/pallas_call | solution.py:356
  (1 shorter events, 0.0 us)
Async XLA Ops:
  0.6 0.7 %copy-start.6 = (f32[1,256]{1,0:T(1,128)S(1)}, f32[1,256]{1,0:T(1,128)}, u32[]{:S(2)}) copy-start(f32[1,256]{1,0:T(1,128)} %param.7) | copy-start | bytes 3076
  0.6 0.7 %copy-start.5 = (f32[1,256]{1,0:T(1,128)S(1)}, f32[1,256]{1,0:T(1,128)}, u32[]{:S(2)}) copy-start(f32[1,256]{1,0:T(1,128)} %param.8) | copy-start | bytes 3076
  2.0 7.3 %copy-start = (f32[32,32]{1,0:T(8,128)S(1)}, f32[32,32]{1,0:T(8,128)}, u32[]{:S(2)}) copy-start(f32[32,32]{1,0:T(8,128)} %kernel_ref.3) | copy-start | bytes 12292
  2.0 7.3 %copy-start.1 = (f32[16,9]{1,0:T(8,128)S(1)}, f32[16,9]{1,0:T(8,128)}, u32[]{:S(2)}) copy-start(f32[16,9]{1,0:T(8,128)} %coupling_ref.1) | copy-start | bytes 1732
  2.0 7.4 %copy-start.4 = (s32[16,8]{0,1:T(8,128)S(1)}, s32[16,8]{0,1:T(8,128)}, u32[]{:S(2)}) copy-start(s32[16,8]{0,1:T(8,128)} %param.11) | copy-start | bytes 1540
  2.0 14.7 %all-to-all-start = ((f32[32,2,256]{2,1,0:T(2,128)}), f32[32,2,256]{2,1,0:T(2,128)S(1)}, u32[]{:S(2)}, u32[]{:S(2)}) async-start(f32[32,2,256]{2,1,0:T(2,128)} %broadcast_in_dim.8), calls=%async_computation | async-start | bytes 131072 | tf_op jit(solution)/shard_map/all_to_all | solution.py:313
  9.4 1.0 %copy-start.2 = (f32[256,256]{1,0:T(8,128)S(1)}, f32[256,256]{1,0:T(8,128)}, u32[]{:S(2)}) copy-start(f32[256,256]{1,0:T(8,128)} %h_ref.5) | copy-start | bytes 786436
  10.3 6.4 %copy-start.3 = (f32[256,256]{1,0:T(8,128)S(1)}, f32[256,256]{1,0:T(8,128)}, u32[]{:S(2)}) copy-start(f32[256,256]{1,0:T(8,128)} %h_ref.5) | copy-start | bytes 786436
  25.2 1.6 %collective-permute-start = (f32[256,256]{1,0:T(8,128)S(1)}, f32[256,256]{1,0:T(8,128)S(1)}, u32[]{:S(2)}, u32[]{:S(2)}) collective-permute-start(f32[256,256]{1,0:T(8,128)S(1)} %get-tuple-element.19), channel_id=1, source_target_pairs={{0,1},{1,0},{2,3},{3,2},{4,5},{5,4},{6,7},{7,6},{8,9},{9,8},{10,11... | collective-permute-start | bytes 786440 | tf_op jit(solution)/shard_map/ppermute | solution.py:337

commit v6 on v5

--- a/solution.py
+++ b/solution.py
@@ -6,7 +6,7 @@
 from jax.sharding import PartitionSpec as P
 
 LANES = 128
-UNROLL = 5
+UNROLL = 15
 
 f32 = jnp.float32
 VMEM = pl.BlockSpec(memory_space=pltpu.VMEM)
@@ -24,6 +24,19 @@
 
 def dot3(a, b, dims=((1,), (0,))):
     return dot(a[0], b[0], dims) + (dot(a[0], b[1], dims) + dot(a[1], b[0], dims))
+
+
+SHARE = 64.0 / 65.0
+
+
+def blend(x):
+    high = x.astype(jnp.bfloat16)
+    low = (x - high.astype(f32)).astype(jnp.bfloat16)
+    return high, low * jnp.bfloat16(8.125) + high * jnp.bfloat16(0.125)
+
+
+def dot2(a, b):
+    return dot(a[0], b[0]) + dot(a[1], b[1])
 
 
 def each(function, *lists):
@@ -69,19 +82,38 @@
     return 2 * lax.rem(me // 2 + jnp.minimum(k, half - 1), half) + lax.rem(me, 2)
 
 
-def weighted(h_ref, rows, columns, scales):
-    norb = h_ref.shape[0]
-    diagonal = eye(norb)
-    sums = series([h_ref[...] * (1.0 / row[:1]) for row in rows])
-    totals = [None] * len(scales)
-    for u, row in enumerate(rows):
-        root = jnp.where(diagonal, 1.0 + sums[u], sums[u]) * columns[u]
-        high, low = split(root * jnp.sqrt(row[1:]))
+def weighted(h_ref, rows, columns, scales, targets):
+    diagonal = eye(h_ref.shape[0])
+
+    def one(row, column, factors):
+        n = h_ref[...] * (SHARE / row[:1])
+        first = split(n)
+        square = dot3(first, first) * (1.0 / SHARE)
+        yield
+        first, second = blend(n), blend(square)
+        cube = dot2(second, first)
+        fourth = dot2(second, second)
+        yield
+        head = n + square + cube
+        rest = dot2(blend(fourth), blend(head))
+        yield
+        s = head + fourth + rest
+        root = jnp.where(diagonal, SHARE + s, s) * column
+        high, low = split(root * (jnp.sqrt(row[1:]) / SHARE))
         flip = ((1,), (1,))
         part = dot(high, high * jnp.bfloat16(0.5), flip) + dot(high, low, flip)
-        for i, scale in enumerate(scales):
-            totals[i] = scale[u] * part if u == 0 else totals[i] + scale[u] * part
-    return totals
+        yield
+        for factor, target in zip(factors, targets):
+            target[...] += factor * part
+
+    waiting = [one(row, columns[u], scales[u]) for u, row in enumerate(rows)]
+    running = []
+    while waiting or running:
+        running += waiting[:1]
+        waiting = waiting[1:]
+        for stages in list(running):
+            if next(stages, 0) == 0:
+                running.remove(stages)
 
 
 def own_kernel(
@@ -94,8 +126,10 @@
     row = row_ref[...]
     column = jnp.broadcast_to(1.0 / row[:1], (8, norb)).T[:, :1]
     me, partner = position()
-    scales = [[kernel_ref[target, me]] for target in (me, partner)]
-    mine_ref[...], other_ref[...] = weighted(h_ref, [row], [column], scales)
+    mine_ref[...] = jnp.zeros_like(mine_ref)
+    other_ref[...] = jnp.zeros_like(other_ref)
+    scales = [kernel_ref[target, me] for target in (me, partner)]
+    weighted(h_ref, [row], [column], [scales], (mine_ref, other_ref))
     half = kernel_ref.shape[0] // 2
     for i, target in enumerate((me, partner)):
         for k in range(1, scales_ref.shape[1]):
@@ -123,10 +157,9 @@
     groups = columns.shape[0]
     unroll = (scales_ref.shape[1] - 1) // groups
     for g in range(groups):
-        rows = [
-            levels_ref[energy_of(1 + g * unroll + u % unroll, half), :1] for u in range(8)
-        ]
-        columns[g, :, :8] = (1.0 / jnp.concatenate(rows, axis=0)).T
+        rows = [levels_ref[energy_of(1 + g * unroll + u, half), :1] for u in range(unroll)]
+        rows += rows[:1] * (-unroll % 8)
+        columns[g, :, : len(rows)] = (1.0 / jnp.concatenate(rows, axis=0)).T
     mine_ref[...] = own_mine_ref[...]
     other_ref[...] = own_other_ref[...]
 
@@ -134,14 +167,13 @@
         ks = [1 + g * unroll + u for u in range(unroll)]
         rows = [levels_ref[energy_of(k, half)] for k in ks]
         scales = [
-            [jnp.concatenate([scales_ref[i, k]] * (norb // LANES), axis=1) for k in ks]
-            for i in range(2)
+            [jnp.concatenate([scales_ref[i, k]] * (norb // LANES), axis=1) for i in range(2)]
+            for k in ks
         ]
-        mine, other = weighted(
-            h_ref, rows, [columns[g, :, u : u + 1] for u in range(unroll)], scales
+        weighted(
+            h_ref, rows, [columns[g, :, u : u + 1] for u in range(unroll)], scales,
+            (mine_ref, other_ref),
         )
-        mine_ref[...] += mine
-        other_ref[...] += other
         return carry
 
     lax.fori_loop(0, groups, group, 0)

time: 50.5 us -> 49.7 us (0.984)
  Pallas kernels: 13.8 us -> 12.9 us
    pallas_call x1, Pallas kernels: 8.41 us -> 7.61 us  [local(): call(first_kernel, (dense, dense), [VMEM] * 5, [pltpu.VMEM((groups, norb,...]
where the time goes in v6:
time: 49.7 us; the launch traced here: 49.4 us
  blocking collectives  20.3 us (41%)
  Pallas kernels  12.9 us (26%)
  starting transfers between devices  7.5 us (15%)
  waiting for transfers between devices  5.57 us (11%)
  local copies, waits for them, and re-layouts  2.29 us (5%)
  between operations  0.72 us (1%)
    all_to_all x2, blocking collectives, exchange(): return lax.all_to_all(x, axes, split_axis=0, concat_axis=0, tiled=True)  20.3 us
    pallas_call x1, Pallas kernels, local(): call(first_kernel, (dense, dense), [VMEM] * 5, [pltpu.VMEM((groups, norb,...  7.61 us
    all_to_all x1, starting transfers between devices, exchange(): return lax.all_to_all(x, axes, split_axis=0, concat_axis=0, tiled=True)  7.33 us
    all_to_all x1, waiting for transfers between devices, exchange(): return lax.all_to_all(x, axes, split_axis=0, concat_axis=0, tiled=True)  4.15 us
    pallas_call x1, Pallas kernels, local(): call(own_kernel, (dense, lanes, scales, dense, dense), [SMEM] * 3 + [VMEM...  2.27 us
    pallas_call x1, Pallas kernels, local(): call(second_kernel, (rows, array(1, norb)), [VMEM] * 6, [scratch], flops=...  1.87 us
    unnamed x14, local copies, waits for them, and re-layouts  1.64 us
    ppermute x1, waiting for transfers between devices, local(): lax.ppermute(other, 'tile', [(i, i + 1 - 2 * (i % 2)) for i in range(tile...  1.42 us
  transfers between devices with their start and end apart: 2, of which 2 were waited for; matrix products, arithmetic and copies ran while one was open for 0% of the time, Pallas kernels for 5%

profile of v6, /device:TPU:0, one launch (start us, length us, event | category | flops | bytes accessed | tf_op | source)
XLA Modules:
  0.0 49.4 jit_solution(8765219205972077476)
XLA Ops:
  0.6 0.0 copy-start.6
  0.6 0.0 copy-start.5
  0.6 0.7 %copy-done.6 = f32[1,256]{1,0:T(1,128)S(1)} copy-done((f32[1,256]{1,0:T(1,128)S(1)}, f32[1,256]{1,0:T(1,128)}, u32[]{:S(2)}) %copy-start.6) | copy-done | bytes 1048
  1.3 0.0 copy-done.5
  1.3 0.6 %broadcast_in_dim.8 = f32[32,2,256]{2,1,0:T(2,128)} broadcast(f32[2,256]{1,0:T(2,128)S(1)} %maximum_bitcast_fusion.row_ref), dimensions={1,2} | broadcast | bytes 67584 | tf_op jit(solution)/shard_map/broadcast_in_dim | solution.py:348
  2.0 0.0 copy-start
  2.0 0.0 copy-start.1
  2.0 0.0 copy-start.4
  2.0 7.3 %all-to-all-start = ((f32[32,2,256]{2,1,0:T(2,128)}), f32[32,2,256]{2,1,0:T(2,128)S(1)}, u32[]{:S(2)}, u32[]{:S(2)}) async-start(f32[32,2,256]{2,1,0:T(2,128)} %broadcast_in_dim.8), calls=%async_computation | async-start | bytes 131072 | tf_op jit(solution)/shard_map/all_to_all | solution.py:345
  9.3 0.0 copy-done
  9.3 0.0 copy-done.1
  9.3 0.0 copy-done.4
  9.4 0.0 copy-start.2
  9.4 0.9 %copy-done.2 = f32[256,256]{1,0:T(8,128)S(1)} copy-done((f32[256,256]{1,0:T(8,128)S(1)}, f32[256,256]{1,0:T(8,128)}, u32[]{:S(2)}) %copy-start.2) | copy-done | bytes 262168
  10.3 0.0 copy-start.3
  10.3 2.3 %shard_map.77 = (f32[256,256]{1,0:T(8,128)S(1)}, s32[16,256]{1,0:T(8,128)S(1)}, f32[2,16,1,128]{3,2,1,0:T(1,128)S(1)}, f32[256,256]{1,0:T(8,128)S(1)}, f32[256,256]{1,0:T(8,128)S(1)}) custom-call(s32[8,16]{1,0:T(8,128)S(1)} %bitcast.16, f32[16,9]{1,0:T(8,128)S(1)} %copy-done.1, f32[32,32]{1,0:T(8,128)S(1)} %copy-done, f32[256,256]{1,0:T(8,128)S(1)} %copy-done.2, ...), custom_call_target="tpu_custom_call" | custom-call | flops 469762048 | bytes 262144 | tf_op jit(solution)/shard_map/pallas_call | solution.py:355
  12.6 4.1 %all-to-all-done.levels_ref = f32[32,2,256]{2,1,0:T(2,128)S(1)} async-done(((f32[32,2,256]{2,1,0:T(2,128)}), f32[32,2,256]{2,1,0:T(2,128)S(1)}, u32[]{:S(2)}, u32[]{:S(2)}) %all-to-all-start) | async-done | bytes 65568 | tf_op jit(solution)/shard_map/all_to_all | solution.py:345
  16.7 0.0 copy-done.3
  16.7 7.6 %shard_map.78 = (f32[256,256]{1,0:T(8,128)S(1)}, f32[256,256]{1,0:T(8,128)S(1)}) custom-call(f32[2,16,1,128]{3,2,1,0:T(1,128)S(1)} %get-tuple-element.15.scales_ref, f32[32,2,256]{2,1,0:T(2,128)S(1)} %all-to-all-done.levels_ref, f32[256,256]{1,0:T(8,128)S(1)} %copy-done.3, f32[256,256]{1,0:T(8,128)S(1)} %get-tuple-element.16.own_mine_ref, ...), custom_call_target="tpu_custom_call" | custom-call | flops 7046430720 | bytes 262144 | tf_op jit(solution)/shard_map/pallas_call | solution.py:361
  24.4 0.2 collective-permute-start
  24.5 1.4 %collective-permute-done.other_ref = f32[256,256]{1,0:T(8,128)S(1)} collective-permute-done((f32[256,256]{1,0:T(8,128)S(1)}, f32[256,256]{1,0:T(8,128)S(1)}, u32[]{:S(2)}, u32[]{:S(2)}) %collective-permute-start) | collective-permute-done | bytes 262176 | tf_op jit(solution)/shard_map/ppermute | solution.py:369
  26.0 1.9 %shard_map.79 = (f32[288,128]{1,0:T(8,128)S(1)}, f32[1,256]{1,0:T(1,128)S(1)}) custom-call(s32[16,256]{1,0:T(8,128)S(1)} %get-tuple-element.13.lanes_ref, f32[256,256]{1,0:T(8,128)S(1)} %get-tuple-element.14.weight_ref, f32[256,256]{1,0:T(8,128)S(1)} %get-tuple-element.18.mine_ref, f32[256,256]{1,0:T(8,128)S(1)} %collective-permute-done.other_ref, ...), custom_call_target="tpu_custom_call" | custom-call | flops 603979776 | bytes 262144 | tf_op jit(solution)/shard_map/pallas_call | solution.py:377
  27.8 10.1 %all_to_all.15 = f32[32,1,1152]{2,1,0:T(1,128)S(1)} all-to-all(f32[32,1,1152]{2,1,0:T(1,128)S(1)} %bitcast.15), channel_id=1, replica_groups=mesh['energy'=8,'tile'=4] {'energy','tile'}, dimensions={0} | all-to-all | bytes 294912 | tf_op jit(solution)/shard_map/all_to_all | solution.py:345
  37.9 0.4 shard_map.80
  38.4 10.2 %all_to_all.16 = f32[32,1,1152]{2,1,0:T(1,128)S(1)} all-to-all(f32[32,1,1152]{2,1,0:T(1,128)S(1)} %bitcast.14), channel_id=1, replica_groups=mesh['energy'=8,'tile'=4] {'energy','tile'}, dimensions={0} | all-to-all | bytes 294912 | tf_op jit(solution)/shard_map/all_to_all | solution.py:345
  48.6 0.8 %shard_map.81 = (f32[9,16,256]{2,1,0:T(8,128)}, f32[1,256]{1,0:T(1,128)}) custom-call(f32[16,9]{1,0:T(8,128)S(1)} %copy-done.1, f32[288,128]{1,0:T(8,128)S(1)} %bitcast.12, f32[1,256]{1,0:T(1,128)S(1)} %get-tuple-element.21.diagonal_ref), custom_call_target="tpu_custom_call" | custom-call | bytes 262144 | tf_op jit(solution)/shard_map/pallas_call | solution.py:388
  (1 shorter events, 0.0 us)
Async XLA Ops:
  0.6 0.7 %copy-start.6 = (f32[1,256]{1,0:T(1,128)S(1)}, f32[1,256]{1,0:T(1,128)}, u32[]{:S(2)}) copy-start(f32[1,256]{1,0:T(1,128)} %param.7) | copy-start | bytes 3076
  0.6 0.7 %copy-start.5 = (f32[1,256]{1,0:T(1,128)S(1)}, f32[1,256]{1,0:T(1,128)}, u32[]{:S(2)}) copy-start(f32[1,256]{1,0:T(1,128)} %param.8) | copy-start | bytes 3076
  2.0 7.3 %copy-start = (f32[32,32]{1,0:T(8,128)S(1)}, f32[32,32]{1,0:T(8,128)}, u32[]{:S(2)}) copy-start(f32[32,32]{1,0:T(8,128)} %kernel_ref.3) | copy-start | bytes 12292
  2.0 7.3 %copy-start.1 = (f32[16,9]{1,0:T(8,128)S(1)}, f32[16,9]{1,0:T(8,128)}, u32[]{:S(2)}) copy-start(f32[16,9]{1,0:T(8,128)} %coupling_ref.1) | copy-start | bytes 1732
  2.0 7.4 %copy-start.4 = (s32[16,8]{0,1:T(8,128)S(1)}, s32[16,8]{0,1:T(8,128)}, u32[]{:S(2)}) copy-start(s32[16,8]{0,1:T(8,128)} %param.11) | copy-start | bytes 1540
  2.0 14.7 %all-to-all-start = ((f32[32,2,256]{2,1,0:T(2,128)}), f32[32,2,256]{2,1,0:T(2,128)S(1)}, u32[]{:S(2)}, u32[]{:S(2)}) async-start(f32[32,2,256]{2,1,0:T(2,128)} %broadcast_in_dim.8), calls=%async_computation | async-start | bytes 131072 | tf_op jit(solution)/shard_map/all_to_all | solution.py:345
  9.4 1.0 %copy-start.2 = (f32[256,256]{1,0:T(8,128)S(1)}, f32[256,256]{1,0:T(8,128)}, u32[]{:S(2)}) copy-start(f32[256,256]{1,0:T(8,128)} %h_ref.5) | copy-start | bytes 786436
  10.3 6.4 %copy-start.3 = (f32[256,256]{1,0:T(8,128)S(1)}, f32[256,256]{1,0:T(8,128)}, u32[]{:S(2)}) copy-start(f32[256,256]{1,0:T(8,128)} %h_ref.5) | copy-start | bytes 786436
  24.4 1.6 %collective-permute-start = (f32[256,256]{1,0:T(8,128)S(1)}, f32[256,256]{1,0:T(8,128)S(1)}, u32[]{:S(2)}, u32[]{:S(2)}) collective-permute-start(f32[256,256]{1,0:T(8,128)S(1)} %get-tuple-element.19), channel_id=1, source_target_pairs={{0,1},{1,0},{2,3},{3,2},{4,5},{5,4},{6,7},{7,6},{8,9},{9,8},{10,11... | collective-permute-start | bytes 786440 | tf_op jit(solution)/shard_map/ppermute | solution.py:369

commit v7 on v6

--- a/solution.py
+++ b/solution.py
@@ -39,19 +39,10 @@
     return dot(a[0], b[0]) + dot(a[1], b[1])
 
 
-def each(function, *lists):
-    return [function(*items) for items in zip(*lists)]
-
-
-def series(ns):
-    first = each(split, ns)
-    squares = each(dot3, first, first)
-    second = each(split, squares)
-    cubes = each(dot3, second, first)
-    heads = each(lambda n, square, cube: n + square + cube, ns, squares, cubes)
-    fourths = each(dot3, second, second)
-    rests = each(dot3, each(split, fourths), each(split, heads))
-    return each(lambda head, fourth, rest: head + fourth + rest, heads, fourths, rests)
+def halves(product, a, *rest):
+    middle = a[0].shape[0] // 2
+    parts = [tuple(x[rows] for x in a) for rows in (slice(0, middle), slice(middle, None))]
+    return jnp.concatenate([product(part, *rest) for part in parts], axis=0)
 
 
 def eye(size):
@@ -187,10 +178,18 @@
     row = row_ref[...]
     inverse_row = 1.0 / row[:1]
     inverse_column = jnp.broadcast_to(inverse_row, (8, norb)).T[:, :1]
-    (s,) = series([(h_ref[...] + sigma) * inverse_row])
-    green = split(jnp.where(diagonal, 1.0 + s, s) * inverse_column)
+    n = (h_ref[...] + sigma) * (SHARE * inverse_row)
+    first = split(n)
+    square = halves(dot3, first, first) * (1.0 / SHARE)
+    first, second = blend(n), blend(square)
+    cube = dot2(second, first)
+    fourth = dot2(second, second)
+    head = n + square + cube
+    s = head + fourth + halves(dot2, blend(fourth), blend(head))
+    green = split(jnp.where(diagonal, SHARE + s, s) * (inverse_column / SHARE))
     source = jnp.where(diagonal, sigma + row[1:], sigma)
-    lesser = dot3(split(dot3(green, split(source))), green, ((1,), (1,)))
+    left = halves(dot3, green, split(source))
+    lesser = halves(dot3, split(left), green, ((1,), (1,)))
     return lesser, jnp.sum(jnp.where(diagonal, lesser, 0.0), axis=0, keepdims=True)
 
 

time: 49.7 us -> 49.5 us (level)
  no operation moved by 1% of the time
where the time goes in v7:
time: 49.5 us; the launch traced here: 49.2 us
  blocking collectives  20.3 us (41%)
  Pallas kernels  12.7 us (26%)
  starting transfers between devices  7.5 us (15%)
  waiting for transfers between devices  5.57 us (11%)
  local copies, waits for them, and re-layouts  2.29 us (5%)
  between operations  0.72 us (1%)
    all_to_all x2, blocking collectives, exchange(): return lax.all_to_all(x, axes, split_axis=0, concat_axis=0, tiled=True)  20.3 us
    pallas_call x1, Pallas kernels, local(): call(first_kernel, (dense, dense), [VMEM] * 5, [pltpu.VMEM((groups, norb,...  7.61 us
    all_to_all x1, starting transfers between devices, exchange(): return lax.all_to_all(x, axes, split_axis=0, concat_axis=0, tiled=True)  7.33 us
    all_to_all x1, waiting for transfers between devices, exchange(): return lax.all_to_all(x, axes, split_axis=0, concat_axis=0, tiled=True)  4.15 us
    pallas_call x1, Pallas kernels, local(): call(own_kernel, (dense, lanes, scales, dense, dense), [SMEM] * 3 + [VMEM...  2.27 us
    pallas_call x1, Pallas kernels, local(): call(second_kernel, (rows, array(1, norb)), [VMEM] * 6, [scratch], flops=...  1.68 us
    unnamed x14, local copies, waits for them, and re-layouts  1.64 us
    ppermute x1, waiting for transfers between devices, local(): lax.ppermute(other, 'tile', [(i, i + 1 - 2 * (i % 2)) for i in range(tile...  1.42 us
  transfers between devices with their start and end apart: 2, of which 2 were waited for; matrix products, arithmetic and copies ran while one was open for 0% of the time, Pallas kernels for 5%

profile of v7, /device:TPU:0, one launch (start us, length us, event | category | flops | bytes accessed | tf_op | source)
XLA Modules:
  0.0 49.2 jit_solution(8808424088370282162)
XLA Ops:
  0.6 0.0 copy-start.6
  0.6 0.0 copy-start.5
  0.6 0.7 %copy-done.6 = f32[1,256]{1,0:T(1,128)S(1)} copy-done((f32[1,256]{1,0:T(1,128)S(1)}, f32[1,256]{1,0:T(1,128)}, u32[]{:S(2)}) %copy-start.6) | copy-done | bytes 1048
  1.3 0.0 copy-done.5
  1.3 0.6 %broadcast_in_dim.8 = f32[32,2,256]{2,1,0:T(2,128)} broadcast(f32[2,256]{1,0:T(2,128)S(1)} %maximum_bitcast_fusion.row_ref), dimensions={1,2} | broadcast | bytes 67584 | tf_op jit(solution)/shard_map/broadcast_in_dim | solution.py:347
  2.0 0.0 copy-start
  2.0 0.0 copy-start.1
  2.0 0.0 copy-start.4
  2.0 7.3 %all-to-all-start = ((f32[32,2,256]{2,1,0:T(2,128)}), f32[32,2,256]{2,1,0:T(2,128)S(1)}, u32[]{:S(2)}, u32[]{:S(2)}) async-start(f32[32,2,256]{2,1,0:T(2,128)} %broadcast_in_dim.8), calls=%async_computation | async-start | bytes 131072 | tf_op jit(solution)/shard_map/all_to_all | solution.py:344
  9.3 0.0 copy-done
  9.3 0.0 copy-done.1
  9.3 0.0 copy-done.4
  9.4 0.0 copy-start.2
  9.4 0.9 %copy-done.2 = f32[256,256]{1,0:T(8,128)S(1)} copy-done((f32[256,256]{1,0:T(8,128)S(1)}, f32[256,256]{1,0:T(8,128)}, u32[]{:S(2)}) %copy-start.2) | copy-done | bytes 262168
  10.3 0.0 copy-start.3
  10.3 2.3 %shard_map.77 = (f32[256,256]{1,0:T(8,128)S(1)}, s32[16,256]{1,0:T(8,128)S(1)}, f32[2,16,1,128]{3,2,1,0:T(1,128)S(1)}, f32[256,256]{1,0:T(8,128)S(1)}, f32[256,256]{1,0:T(8,128)S(1)}) custom-call(s32[8,16]{1,0:T(8,128)S(1)} %bitcast.16, f32[16,9]{1,0:T(8,128)S(1)} %copy-done.1, f32[32,32]{1,0:T(8,128)S(1)} %copy-done, f32[256,256]{1,0:T(8,128)S(1)} %copy-done.2, ...), custom_call_target="tpu_custom_call" | custom-call | flops 469762048 | bytes 262144 | tf_op jit(solution)/shard_map/pallas_call | solution.py:354
  12.6 4.1 %all-to-all-done.levels_ref = f32[32,2,256]{2,1,0:T(2,128)S(1)} async-done(((f32[32,2,256]{2,1,0:T(2,128)}), f32[32,2,256]{2,1,0:T(2,128)S(1)}, u32[]{:S(2)}, u32[]{:S(2)}) %all-to-all-start) | async-done | bytes 65568 | tf_op jit(solution)/shard_map/all_to_all | solution.py:344
  16.7 0.0 copy-done.3
  16.7 7.6 %shard_map.78 = (f32[256,256]{1,0:T(8,128)S(1)}, f32[256,256]{1,0:T(8,128)S(1)}) custom-call(f32[2,16,1,128]{3,2,1,0:T(1,128)S(1)} %get-tuple-element.15.scales_ref, f32[32,2,256]{2,1,0:T(2,128)S(1)} %all-to-all-done.levels_ref, f32[256,256]{1,0:T(8,128)S(1)} %copy-done.3, f32[256,256]{1,0:T(8,128)S(1)} %get-tuple-element.16.own_mine_ref, ...), custom_call_target="tpu_custom_call" | custom-call | flops 7046430720 | bytes 262144 | tf_op jit(solution)/shard_map/pallas_call | solution.py:360
  24.4 0.2 collective-permute-start
  24.5 1.4 %collective-permute-done.other_ref = f32[256,256]{1,0:T(8,128)S(1)} collective-permute-done((f32[256,256]{1,0:T(8,128)S(1)}, f32[256,256]{1,0:T(8,128)S(1)}, u32[]{:S(2)}, u32[]{:S(2)}) %collective-permute-start) | collective-permute-done | bytes 262176 | tf_op jit(solution)/shard_map/ppermute | solution.py:368
  26.0 1.7 %shard_map.79 = (f32[288,128]{1,0:T(8,128)S(1)}, f32[1,256]{1,0:T(1,128)S(1)}) custom-call(s32[16,256]{1,0:T(8,128)S(1)} %get-tuple-element.13.lanes_ref, f32[256,256]{1,0:T(8,128)S(1)} %get-tuple-element.14.weight_ref, f32[256,256]{1,0:T(8,128)S(1)} %get-tuple-element.18.mine_ref, f32[256,256]{1,0:T(8,128)S(1)} %collective-permute-done.other_ref, ...), custom_call_target="tpu_custom_call" | custom-call | flops 603979776 | bytes 262144 | tf_op jit(solution)/shard_map/pallas_call | solution.py:376
  27.6 10.1 %all_to_all.15 = f32[32,1,1152]{2,1,0:T(1,128)S(1)} all-to-all(f32[32,1,1152]{2,1,0:T(1,128)S(1)} %bitcast.15), channel_id=1, replica_groups=mesh['energy'=8,'tile'=4] {'energy','tile'}, dimensions={0} | all-to-all | bytes 294912 | tf_op jit(solution)/shard_map/all_to_all | solution.py:344
  37.8 0.4 shard_map.80
  38.2 10.2 %all_to_all.16 = f32[32,1,1152]{2,1,0:T(1,128)S(1)} all-to-all(f32[32,1,1152]{2,1,0:T(1,128)S(1)} %bitcast.14), channel_id=1, replica_groups=mesh['energy'=8,'tile'=4] {'energy','tile'}, dimensions={0} | all-to-all | bytes 294912 | tf_op jit(solution)/shard_map/all_to_all | solution.py:344
  48.4 0.8 %shard_map.81 = (f32[9,16,256]{2,1,0:T(8,128)}, f32[1,256]{1,0:T(1,128)}) custom-call(f32[16,9]{1,0:T(8,128)S(1)} %copy-done.1, f32[288,128]{1,0:T(8,128)S(1)} %bitcast.12, f32[1,256]{1,0:T(1,128)S(1)} %get-tuple-element.21.diagonal_ref), custom_call_target="tpu_custom_call" | custom-call | bytes 262144 | tf_op jit(solution)/shard_map/pallas_call | solution.py:387
  (1 shorter events, 0.0 us)
Async XLA Ops:
  0.6 0.7 %copy-start.6 = (f32[1,256]{1,0:T(1,128)S(1)}, f32[1,256]{1,0:T(1,128)}, u32[]{:S(2)}) copy-start(f32[1,256]{1,0:T(1,128)} %param.7) | copy-start | bytes 3076
  0.6 0.7 %copy-start.5 = (f32[1,256]{1,0:T(1,128)S(1)}, f32[1,256]{1,0:T(1,128)}, u32[]{:S(2)}) copy-start(f32[1,256]{1,0:T(1,128)} %param.8) | copy-start | bytes 3076
  2.0 7.3 %copy-start = (f32[32,32]{1,0:T(8,128)S(1)}, f32[32,32]{1,0:T(8,128)}, u32[]{:S(2)}) copy-start(f32[32,32]{1,0:T(8,128)} %kernel_ref.3) | copy-start | bytes 12292
  2.0 7.3 %copy-start.1 = (f32[16,9]{1,0:T(8,128)S(1)}, f32[16,9]{1,0:T(8,128)}, u32[]{:S(2)}) copy-start(f32[16,9]{1,0:T(8,128)} %coupling_ref.1) | copy-start | bytes 1732
  2.0 7.4 %copy-start.4 = (s32[16,8]{0,1:T(8,128)S(1)}, s32[16,8]{0,1:T(8,128)}, u32[]{:S(2)}) copy-start(s32[16,8]{0,1:T(8,128)} %param.11) | copy-start | bytes 1540
  2.0 14.7 %all-to-all-start = ((f32[32,2,256]{2,1,0:T(2,128)}), f32[32,2,256]{2,1,0:T(2,128)S(1)}, u32[]{:S(2)}, u32[]{:S(2)}) async-start(f32[32,2,256]{2,1,0:T(2,128)} %broadcast_in_dim.8), calls=%async_computation | async-start | bytes 131072 | tf_op jit(solution)/shard_map/all_to_all | solution.py:344
  9.4 1.0 %copy-start.2 = (f32[256,256]{1,0:T(8,128)S(1)}, f32[256,256]{1,0:T(8,128)}, u32[]{:S(2)}) copy-start(f32[256,256]{1,0:T(8,128)} %h_ref.5) | copy-start | bytes 786436
  10.3 6.4 %copy-start.3 = (f32[256,256]{1,0:T(8,128)S(1)}, f32[256,256]{1,0:T(8,128)}, u32[]{:S(2)}) copy-start(f32[256,256]{1,0:T(8,128)} %h_ref.5) | copy-start | bytes 786436
  24.4 1.6 %collective-permute-start = (f32[256,256]{1,0:T(8,128)S(1)}, f32[256,256]{1,0:T(8,128)S(1)}, u32[]{:S(2)}, u32[]{:S(2)}) collective-permute-start(f32[256,256]{1,0:T(8,128)S(1)} %get-tuple-element.19), channel_id=1, source_target_pairs={{0,1},{1,0},{2,3},{3,2},{4,5},{5,4},{6,7},{7,6},{8,9},{9,8},{10,11... | collective-permute-start | bytes 786440 | tf_op jit(solution)/shard_map/ppermute | solution.py:368

commit v8 on v7

--- a/solution.py
+++ b/solution.py
@@ -178,15 +178,15 @@
     row = row_ref[...]
     inverse_row = 1.0 / row[:1]
     inverse_column = jnp.broadcast_to(inverse_row, (8, norb)).T[:, :1]
-    n = (h_ref[...] + sigma) * (SHARE * inverse_row)
+    n = (h_ref[...] + sigma) * inverse_row
     first = split(n)
-    square = halves(dot3, first, first) * (1.0 / SHARE)
-    first, second = blend(n), blend(square)
-    cube = dot2(second, first)
-    fourth = dot2(second, second)
+    square = halves(dot3, first, first)
+    second = split(square)
+    cube = dot3(second, first)
+    fourth = dot3(second, second)
     head = n + square + cube
-    s = head + fourth + halves(dot2, blend(fourth), blend(head))
-    green = split(jnp.where(diagonal, SHARE + s, s) * (inverse_column / SHARE))
+    s = head + fourth + halves(dot3, split(fourth), split(head))
+    green = split(jnp.where(diagonal, 1.0 + s, s) * inverse_column)
     source = jnp.where(diagonal, sigma + row[1:], sigma)
     left = halves(dot3, green, split(source))
     lesser = halves(dot3, split(left), green, ((1,), (1,)))

time: 49.5 us -> 49.6 us (level)
  no operation moved by 1% of the time
where the time goes in v8:
time: 49.6 us; the launch traced here: 49.3 us
  blocking collectives  20.3 us (41%)
  Pallas kernels  12.8 us (26%)
  starting transfers between devices  7.5 us (15%)
  waiting for transfers between devices  5.57 us (11%)
  local copies, waits for them, and re-layouts  2.29 us (5%)
  between operations  0.72 us (1%)
    all_to_all x2, blocking collectives, exchange(): return lax.all_to_all(x, axes, split_axis=0, concat_axis=0, tiled=True)  20.3 us
    pallas_call x1, Pallas kernels, local(): call(first_kernel, (dense, dense), [VMEM] * 5, [pltpu.VMEM((groups, norb,...  7.61 us
    all_to_all x1, starting transfers between devices, exchange(): return lax.all_to_all(x, axes, split_axis=0, concat_axis=0, tiled=True)  7.33 us
    all_to_all x1, waiting for transfers between devices, exchange(): return lax.all_to_all(x, axes, split_axis=0, concat_axis=0, tiled=True)  4.15 us
    pallas_call x1, Pallas kernels, local(): call(own_kernel, (dense, lanes, scales, dense, dense), [SMEM] * 3 + [VMEM...  2.27 us
    pallas_call x1, Pallas kernels, local(): call(second_kernel, (rows, array(1, norb)), [VMEM] * 6, [scratch], flops=...  1.76 us
    unnamed x14, local copies, waits for them, and re-layouts  1.64 us
    ppermute x1, waiting for transfers between devices, local(): lax.ppermute(other, 'tile', [(i, i + 1 - 2 * (i % 2)) for i in range(tile...  1.42 us
  transfers between devices with their start and end apart: 2, of which 2 were waited for; matrix products, arithmetic and copies ran while one was open for 0% of the time, Pallas kernels for 5%

profile of v8, /device:TPU:0, one launch (start us, length us, event | category | flops | bytes accessed | tf_op | source)
XLA Modules:
  0.0 49.3 jit_solution(14098535198865044855)
XLA Ops:
  0.6 0.0 copy-start.6
  0.6 0.0 copy-start.5
  0.6 0.7 %copy-done.6 = f32[1,256]{1,0:T(1,128)S(1)} copy-done((f32[1,256]{1,0:T(1,128)S(1)}, f32[1,256]{1,0:T(1,128)}, u32[]{:S(2)}) %copy-start.6) | copy-done | bytes 1048
  1.3 0.0 copy-done.5
  1.3 0.6 %broadcast_in_dim.8 = f32[32,2,256]{2,1,0:T(2,128)} broadcast(f32[2,256]{1,0:T(2,128)S(1)} %maximum_bitcast_fusion.row_ref), dimensions={1,2} | broadcast | bytes 67584 | tf_op jit(solution)/shard_map/broadcast_in_dim | solution.py:347
  2.0 0.0 copy-start
  2.0 0.0 copy-start.1
  2.0 0.0 copy-start.4
  2.0 7.3 %all-to-all-start = ((f32[32,2,256]{2,1,0:T(2,128)}), f32[32,2,256]{2,1,0:T(2,128)S(1)}, u32[]{:S(2)}, u32[]{:S(2)}) async-start(f32[32,2,256]{2,1,0:T(2,128)} %broadcast_in_dim.8), calls=%async_computation | async-start | bytes 131072 | tf_op jit(solution)/shard_map/all_to_all | solution.py:344
  9.3 0.0 copy-done
  9.3 0.0 copy-done.1
  9.3 0.0 copy-done.4
  9.4 0.0 copy-start.2
  9.4 0.9 %copy-done.2 = f32[256,256]{1,0:T(8,128)S(1)} copy-done((f32[256,256]{1,0:T(8,128)S(1)}, f32[256,256]{1,0:T(8,128)}, u32[]{:S(2)}) %copy-start.2) | copy-done | bytes 262168
  10.3 0.0 copy-start.3
  10.3 2.3 %shard_map.77 = (f32[256,256]{1,0:T(8,128)S(1)}, s32[16,256]{1,0:T(8,128)S(1)}, f32[2,16,1,128]{3,2,1,0:T(1,128)S(1)}, f32[256,256]{1,0:T(8,128)S(1)}, f32[256,256]{1,0:T(8,128)S(1)}) custom-call(s32[8,16]{1,0:T(8,128)S(1)} %bitcast.16, f32[16,9]{1,0:T(8,128)S(1)} %copy-done.1, f32[32,32]{1,0:T(8,128)S(1)} %copy-done, f32[256,256]{1,0:T(8,128)S(1)} %copy-done.2, ...), custom_call_target="tpu_custom_call" | custom-call | flops 469762048 | bytes 262144 | tf_op jit(solution)/shard_map/pallas_call | solution.py:354
  12.6 4.1 %all-to-all-done.levels_ref = f32[32,2,256]{2,1,0:T(2,128)S(1)} async-done(((f32[32,2,256]{2,1,0:T(2,128)}), f32[32,2,256]{2,1,0:T(2,128)S(1)}, u32[]{:S(2)}, u32[]{:S(2)}) %all-to-all-start) | async-done | bytes 65568 | tf_op jit(solution)/shard_map/all_to_all | solution.py:344
  16.7 0.0 copy-done.3
  16.7 7.6 %shard_map.78 = (f32[256,256]{1,0:T(8,128)S(1)}, f32[256,256]{1,0:T(8,128)S(1)}) custom-call(f32[2,16,1,128]{3,2,1,0:T(1,128)S(1)} %get-tuple-element.15.scales_ref, f32[32,2,256]{2,1,0:T(2,128)S(1)} %all-to-all-done.levels_ref, f32[256,256]{1,0:T(8,128)S(1)} %copy-done.3, f32[256,256]{1,0:T(8,128)S(1)} %get-tuple-element.16.own_mine_ref, ...), custom_call_target="tpu_custom_call" | custom-call | flops 7046430720 | bytes 262144 | tf_op jit(solution)/shard_map/pallas_call | solution.py:360
  24.4 0.2 collective-permute-start
  24.5 1.4 %collective-permute-done.other_ref = f32[256,256]{1,0:T(8,128)S(1)} collective-permute-done((f32[256,256]{1,0:T(8,128)S(1)}, f32[256,256]{1,0:T(8,128)S(1)}, u32[]{:S(2)}, u32[]{:S(2)}) %collective-permute-start) | collective-permute-done | bytes 262176 | tf_op jit(solution)/shard_map/ppermute | solution.py:368
  26.0 1.8 %shard_map.79 = (f32[288,128]{1,0:T(8,128)S(1)}, f32[1,256]{1,0:T(1,128)S(1)}) custom-call(s32[16,256]{1,0:T(8,128)S(1)} %get-tuple-element.13.lanes_ref, f32[256,256]{1,0:T(8,128)S(1)} %get-tuple-element.14.weight_ref, f32[256,256]{1,0:T(8,128)S(1)} %get-tuple-element.18.mine_ref, f32[256,256]{1,0:T(8,128)S(1)} %collective-permute-done.other_ref, ...), custom_call_target="tpu_custom_call" | custom-call | flops 603979776 | bytes 262144 | tf_op jit(solution)/shard_map/pallas_call | solution.py:376
  27.7 10.1 %all_to_all.15 = f32[32,1,1152]{2,1,0:T(1,128)S(1)} all-to-all(f32[32,1,1152]{2,1,0:T(1,128)S(1)} %bitcast.15), channel_id=1, replica_groups=mesh['energy'=8,'tile'=4] {'energy','tile'}, dimensions={0} | all-to-all | bytes 294912 | tf_op jit(solution)/shard_map/all_to_all | solution.py:344
  37.8 0.4 shard_map.80
  38.3 10.2 %all_to_all.16 = f32[32,1,1152]{2,1,0:T(1,128)S(1)} all-to-all(f32[32,1,1152]{2,1,0:T(1,128)S(1)} %bitcast.14), channel_id=1, replica_groups=mesh['energy'=8,'tile'=4] {'energy','tile'}, dimensions={0} | all-to-all | bytes 294912 | tf_op jit(solution)/shard_map/all_to_all | solution.py:344
  48.5 0.8 %shard_map.81 = (f32[9,16,256]{2,1,0:T(8,128)}, f32[1,256]{1,0:T(1,128)}) custom-call(f32[16,9]{1,0:T(8,128)S(1)} %copy-done.1, f32[288,128]{1,0:T(8,128)S(1)} %bitcast.12, f32[1,256]{1,0:T(1,128)S(1)} %get-tuple-element.21.diagonal_ref), custom_call_target="tpu_custom_call" | custom-call | bytes 262144 | tf_op jit(solution)/shard_map/pallas_call | solution.py:387
  (1 shorter events, 0.0 us)
Async XLA Ops:
  0.6 0.7 %copy-start.6 = (f32[1,256]{1,0:T(1,128)S(1)}, f32[1,256]{1,0:T(1,128)}, u32[]{:S(2)}) copy-start(f32[1,256]{1,0:T(1,128)} %param.7) | copy-start | bytes 3076
  0.6 0.7 %copy-start.5 = (f32[1,256]{1,0:T(1,128)S(1)}, f32[1,256]{1,0:T(1,128)}, u32[]{:S(2)}) copy-start(f32[1,256]{1,0:T(1,128)} %param.8) | copy-start | bytes 3076
  2.0 7.3 %copy-start = (f32[32,32]{1,0:T(8,128)S(1)}, f32[32,32]{1,0:T(8,128)}, u32[]{:S(2)}) copy-start(f32[32,32]{1,0:T(8,128)} %kernel_ref.3) | copy-start | bytes 12292
  2.0 7.3 %copy-start.1 = (f32[16,9]{1,0:T(8,128)S(1)}, f32[16,9]{1,0:T(8,128)}, u32[]{:S(2)}) copy-start(f32[16,9]{1,0:T(8,128)} %coupling_ref.1) | copy-start | bytes 1732
  2.0 7.4 %copy-start.4 = (s32[16,8]{0,1:T(8,128)S(1)}, s32[16,8]{0,1:T(8,128)}, u32[]{:S(2)}) copy-start(s32[16,8]{0,1:T(8,128)} %param.11) | copy-start | bytes 1540
  2.0 14.7 %all-to-all-start = ((f32[32,2,256]{2,1,0:T(2,128)}), f32[32,2,256]{2,1,0:T(2,128)S(1)}, u32[]{:S(2)}, u32[]{:S(2)}) async-start(f32[32,2,256]{2,1,0:T(2,128)} %broadcast_in_dim.8), calls=%async_computation | async-start | bytes 131072 | tf_op jit(solution)/shard_map/all_to_all | solution.py:344
  9.4 1.0 %copy-start.2 = (f32[256,256]{1,0:T(8,128)S(1)}, f32[256,256]{1,0:T(8,128)}, u32[]{:S(2)}) copy-start(f32[256,256]{1,0:T(8,128)} %h_ref.5) | copy-start | bytes 786436
  10.3 6.4 %copy-start.3 = (f32[256,256]{1,0:T(8,128)S(1)}, f32[256,256]{1,0:T(8,128)}, u32[]{:S(2)}) copy-start(f32[256,256]{1,0:T(8,128)} %h_ref.5) | copy-start | bytes 786436
  24.4 1.6 %collective-permute-start = (f32[256,256]{1,0:T(8,128)S(1)}, f32[256,256]{1,0:T(8,128)S(1)}, u32[]{:S(2)}, u32[]{:S(2)}) collective-permute-start(f32[256,256]{1,0:T(8,128)S(1)} %get-tuple-element.19), channel_id=1, source_target_pairs={{0,1},{1,0},{2,3},{3,2},{4,5},{5,4},{6,7},{7,6},{8,9},{9,8},{10,11... | collective-permute-start | bytes 786440 | tf_op jit(solution)/shard_map/ppermute | solution.py:368

commit v9 on v8

--- a/solution.py
+++ b/solution.py
@@ -73,10 +73,14 @@
     return 2 * lax.rem(me // 2 + jnp.minimum(k, half - 1), half) + lax.rem(me, 2)
 
 
-def weighted(h_ref, rows, columns, scales, targets):
+def column(row):
+    return jnp.broadcast_to(row, (8, row.shape[1])).T[:, :1]
+
+
+def weighted(h_ref, rows, scales, bases, targets):
     diagonal = eye(h_ref.shape[0])
 
-    def one(row, column, factors):
+    def one(row, factors, bases):
         n = h_ref[...] * (SHARE / row[:1])
         first = split(n)
         square = dot3(first, first) * (1.0 / SHARE)
@@ -89,15 +93,15 @@
         rest = dot2(blend(fourth), blend(head))
         yield
         s = head + fourth + rest
-        root = jnp.where(diagonal, SHARE + s, s) * column
+        root = jnp.where(diagonal, SHARE + s, s) * column(1.0 / row[:1])
         high, low = split(root * (jnp.sqrt(row[1:]) / SHARE))
         flip = ((1,), (1,))
         part = dot(high, high * jnp.bfloat16(0.5), flip) + dot(high, low, flip)
         yield
-        for factor, target in zip(factors, targets):
-            target[...] += factor * part
-
-    waiting = [one(row, columns[u], scales[u]) for u, row in enumerate(rows)]
+        for factor, base, target in zip(factors, bases, targets):
+            target[...] = base[...] + factor * part
+
+    waiting = [one(row, scales[u], targets if u else bases) for u, row in enumerate(rows)]
     running = []
     while waiting or running:
         running += waiting[:1]
@@ -115,12 +119,12 @@
     norb = weight_ref.shape[0]
     b = norb // tiles
     row = row_ref[...]
-    column = jnp.broadcast_to(1.0 / row[:1], (8, norb)).T[:, :1]
     me, partner = position()
     mine_ref[...] = jnp.zeros_like(mine_ref)
     other_ref[...] = jnp.zeros_like(other_ref)
     scales = [kernel_ref[target, me] for target in (me, partner)]
-    weighted(h_ref, [row], [column], [scales], (mine_ref, other_ref))
+    targets = (mine_ref, other_ref)
+    weighted(h_ref, [row], [scales], targets, targets)
     half = kernel_ref.shape[0] // 2
     for i, target in enumerate((me, partner)):
         for k in range(1, scales_ref.shape[1]):
@@ -141,18 +145,17 @@
 
 
 def first_kernel(
-    scales_ref, levels_ref, h_ref, own_mine_ref, own_other_ref, mine_ref, other_ref, columns
+    scales_ref, levels_ref, h_ref, own_mine_ref, own_other_ref, mine_ref, other_ref
 ):
     norb = h_ref.shape[0]
     half = levels_ref.shape[0] // 2
-    groups = columns.shape[0]
+    groups = -(-(half - 1) // UNROLL)
     unroll = (scales_ref.shape[1] - 1) // groups
-    for g in range(groups):
-        rows = [levels_ref[energy_of(1 + g * unroll + u, half), :1] for u in range(unroll)]
-        rows += rows[:1] * (-unroll % 8)
-        columns[g, :, : len(rows)] = (1.0 / jnp.concatenate(rows, axis=0)).T
-    mine_ref[...] = own_mine_ref[...]
-    other_ref[...] = own_other_ref[...]
+    bases, targets = (own_mine_ref, own_other_ref), (mine_ref, other_ref)
+    if groups > 1:
+        mine_ref[...] = own_mine_ref[...]
+        other_ref[...] = own_other_ref[...]
+        bases = targets
 
     def group(g, carry):
         ks = [1 + g * unroll + u for u in range(unroll)]
@@ -161,10 +164,7 @@
             [jnp.concatenate([scales_ref[i, k]] * (norb // LANES), axis=1) for i in range(2)]
             for k in ks
         ]
-        weighted(
-            h_ref, rows, [columns[g, :, u : u + 1] for u in range(unroll)], scales,
-            (mine_ref, other_ref),
-        )
+        weighted(h_ref, rows, scales, bases, targets)
         return carry
 
     lax.fori_loop(0, groups, group, 0)
@@ -177,7 +177,7 @@
     diagonal = eye(norb)
     row = row_ref[...]
     inverse_row = 1.0 / row[:1]
-    inverse_column = jnp.broadcast_to(inverse_row, (8, norb)).T[:, :1]
+    inverse_column = column(inverse_row)
     n = (h_ref[...] + sigma) * inverse_row
     first = split(n)
     square = halves(dot3, first, first)
@@ -361,7 +361,6 @@
         first_kernel,
         (dense, dense),
         [VMEM] * 5,
-        [pltpu.VMEM((groups, norb, LANES), f32)],
         vmem=24,
         flops=(half - 1) * energy_flops,
     )(scales, all_levels, hamiltonian, mine, other)

time: 49.6 us -> 49.5 us (level)
  no operation moved by 1% of the time
where the time goes in v9:
time: 49.5 us; the launch traced here: 49.2 us
  blocking collectives  20.3 us (41%)
  Pallas kernels  12.8 us (26%)
  starting transfers between devices  7.51 us (15%)
  waiting for transfers between devices  5.57 us (11%)
  local copies, waits for them, and re-layouts  2.29 us (5%)
  between operations  0.72 us (1%)
    all_to_all x2, blocking collectives, exchange(): return lax.all_to_all(x, axes, split_axis=0, concat_axis=0, tiled=True)  20.3 us
    pallas_call x1, Pallas kernels, local(): call(first_kernel, (dense, dense), [VMEM] * 5, vmem=24, flops=(half - 1)...  7.55 us
    all_to_all x1, starting transfers between devices, exchange(): return lax.all_to_all(x, axes, split_axis=0, concat_axis=0, tiled=True)  7.33 us
    all_to_all x1, waiting for transfers between devices, exchange(): return lax.all_to_all(x, axes, split_axis=0, concat_axis=0, tiled=True)  4.15 us
    pallas_call x1, Pallas kernels, local(): call(own_kernel, (dense, lanes, scales, dense, dense), [SMEM] * 3 + [VMEM...  2.27 us
    pallas_call x1, Pallas kernels, local(): call(second_kernel, (rows, array(1, norb)), [VMEM] * 6, [scratch], flops=...  1.75 us
    unnamed x14, local copies, waits for them, and re-layouts  1.64 us
    ppermute x1, waiting for transfers between devices, local(): lax.ppermute(other, 'tile', [(i, i + 1 - 2 * (i % 2)) for i in range(tile...  1.42 us
  transfers between devices with their start and end apart: 2, of which 2 were waited for; matrix products, arithmetic and copies ran while one was open for 0% of the time, Pallas kernels for 5%

profile of v9, /device:TPU:0, one launch (start us, length us, event | category | flops | bytes accessed | tf_op | source)
XLA Modules:
  0.0 49.2 jit_solution(7993113923361371006)
XLA Ops:
  0.6 0.0 copy-start.6
  0.6 0.0 copy-start.5
  0.6 0.7 %copy-done.6 = f32[1,256]{1,0:T(1,128)S(1)} copy-done((f32[1,256]{1,0:T(1,128)S(1)}, f32[1,256]{1,0:T(1,128)}, u32[]{:S(2)}) %copy-start.6) | copy-done | bytes 1048
  1.3 0.0 copy-done.5
  1.3 0.6 %broadcast_in_dim.8 = f32[32,2,256]{2,1,0:T(2,128)} broadcast(f32[2,256]{1,0:T(2,128)S(1)} %maximum_bitcast_fusion.row_ref), dimensions={1,2} | broadcast | bytes 67584 | tf_op jit(solution)/shard_map/broadcast_in_dim | solution.py:347
  2.0 0.0 copy-start
  2.0 0.0 copy-start.1
  2.0 0.0 copy-start.4
  2.0 7.3 %all-to-all-start = ((f32[32,2,256]{2,1,0:T(2,128)}), f32[32,2,256]{2,1,0:T(2,128)S(1)}, u32[]{:S(2)}, u32[]{:S(2)}) async-start(f32[32,2,256]{2,1,0:T(2,128)} %broadcast_in_dim.8), calls=%async_computation | async-start | bytes 131072 | tf_op jit(solution)/shard_map/all_to_all | solution.py:344
  9.3 0.0 copy-done
  9.3 0.0 copy-done.1
  9.3 0.0 copy-done.4
  9.4 0.0 copy-start.2
  9.4 0.9 %copy-done.2 = f32[256,256]{1,0:T(8,128)S(1)} copy-done((f32[256,256]{1,0:T(8,128)S(1)}, f32[256,256]{1,0:T(8,128)}, u32[]{:S(2)}) %copy-start.2) | copy-done | bytes 262168
  10.3 0.0 copy-start.3
  10.3 2.3 %shard_map.77 = (f32[256,256]{1,0:T(8,128)S(1)}, s32[16,256]{1,0:T(8,128)S(1)}, f32[2,16,1,128]{3,2,1,0:T(1,128)S(1)}, f32[256,256]{1,0:T(8,128)S(1)}, f32[256,256]{1,0:T(8,128)S(1)}) custom-call(s32[8,16]{1,0:T(8,128)S(1)} %bitcast.16, f32[16,9]{1,0:T(8,128)S(1)} %copy-done.1, f32[32,32]{1,0:T(8,128)S(1)} %copy-done, f32[256,256]{1,0:T(8,128)S(1)} %copy-done.2, ...), custom_call_target="tpu_custom_call" | custom-call | flops 469762048 | bytes 262144 | tf_op jit(solution)/shard_map/pallas_call | solution.py:354
  12.6 4.1 %all-to-all-done.levels_ref = f32[32,2,256]{2,1,0:T(2,128)S(1)} async-done(((f32[32,2,256]{2,1,0:T(2,128)}), f32[32,2,256]{2,1,0:T(2,128)S(1)}, u32[]{:S(2)}, u32[]{:S(2)}) %all-to-all-start) | async-done | bytes 65568 | tf_op jit(solution)/shard_map/all_to_all | solution.py:344
  16.7 0.0 copy-done.3
  16.7 7.6 %shard_map.78 = (f32[256,256]{1,0:T(8,128)S(1)}, f32[256,256]{1,0:T(8,128)S(1)}) custom-call(f32[2,16,1,128]{3,2,1,0:T(1,128)S(1)} %get-tuple-element.15.scales_ref, f32[32,2,256]{2,1,0:T(2,128)S(1)} %all-to-all-done.levels_ref, f32[256,256]{1,0:T(8,128)S(1)} %copy-done.3, f32[256,256]{1,0:T(8,128)S(1)} %get-tuple-element.16.own_mine_ref, ...), custom_call_target="tpu_custom_call" | custom-call | flops 7046430720 | bytes 262144 | tf_op jit(solution)/shard_map/pallas_call | solution.py:360
  24.3 0.2 collective-permute-start
  24.5 1.4 %collective-permute-done.other_ref = f32[256,256]{1,0:T(8,128)S(1)} collective-permute-done((f32[256,256]{1,0:T(8,128)S(1)}, f32[256,256]{1,0:T(8,128)S(1)}, u32[]{:S(2)}, u32[]{:S(2)}) %collective-permute-start) | collective-permute-done | bytes 262176 | tf_op jit(solution)/shard_map/ppermute | solution.py:367
  25.9 1.8 %shard_map.79 = (f32[288,128]{1,0:T(8,128)S(1)}, f32[1,256]{1,0:T(1,128)S(1)}) custom-call(s32[16,256]{1,0:T(8,128)S(1)} %get-tuple-element.13.lanes_ref, f32[256,256]{1,0:T(8,128)S(1)} %get-tuple-element.14.weight_ref, f32[256,256]{1,0:T(8,128)S(1)} %get-tuple-element.18.mine_ref, f32[256,256]{1,0:T(8,128)S(1)} %collective-permute-done.other_ref, ...), custom_call_target="tpu_custom_call" | custom-call | flops 603979776 | bytes 262144 | tf_op jit(solution)/shard_map/pallas_call | solution.py:375
  27.7 10.1 %all_to_all.15 = f32[32,1,1152]{2,1,0:T(1,128)S(1)} all-to-all(f32[32,1,1152]{2,1,0:T(1,128)S(1)} %bitcast.15), channel_id=1, replica_groups=mesh['energy'=8,'tile'=4] {'energy','tile'}, dimensions={0} | all-to-all | bytes 294912 | tf_op jit(solution)/shard_map/all_to_all | solution.py:344
  37.8 0.4 shard_map.80
  38.2 10.2 %all_to_all.16 = f32[32,1,1152]{2,1,0:T(1,128)S(1)} all-to-all(f32[32,1,1152]{2,1,0:T(1,128)S(1)} %bitcast.14), channel_id=1, replica_groups=mesh['energy'=8,'tile'=4] {'energy','tile'}, dimensions={0} | all-to-all | bytes 294912 | tf_op jit(solution)/shard_map/all_to_all | solution.py:344
  48.4 0.8 %shard_map.81 = (f32[9,16,256]{2,1,0:T(8,128)}, f32[1,256]{1,0:T(1,128)}) custom-call(f32[16,9]{1,0:T(8,128)S(1)} %copy-done.1, f32[288,128]{1,0:T(8,128)S(1)} %bitcast.12, f32[1,256]{1,0:T(1,128)S(1)} %get-tuple-element.21.diagonal_ref), custom_call_target="tpu_custom_call" | custom-call | bytes 262144 | tf_op jit(solution)/shard_map/pallas_call | solution.py:386
  (1 shorter events, 0.0 us)
Async XLA Ops:
  0.6 0.7 %copy-start.6 = (f32[1,256]{1,0:T(1,128)S(1)}, f32[1,256]{1,0:T(1,128)}, u32[]{:S(2)}) copy-start(f32[1,256]{1,0:T(1,128)} %param.7) | copy-start | bytes 3076
  0.6 0.7 %copy-start.5 = (f32[1,256]{1,0:T(1,128)S(1)}, f32[1,256]{1,0:T(1,128)}, u32[]{:S(2)}) copy-start(f32[1,256]{1,0:T(1,128)} %param.8) | copy-start | bytes 3076
  2.0 7.3 %copy-start = (f32[32,32]{1,0:T(8,128)S(1)}, f32[32,32]{1,0:T(8,128)}, u32[]{:S(2)}) copy-start(f32[32,32]{1,0:T(8,128)} %kernel_ref.3) | copy-start | bytes 12292
  2.0 7.3 %copy-start.1 = (f32[16,9]{1,0:T(8,128)S(1)}, f32[16,9]{1,0:T(8,128)}, u32[]{:S(2)}) copy-start(f32[16,9]{1,0:T(8,128)} %coupling_ref.1) | copy-start | bytes 1732
  2.0 7.4 %copy-start.4 = (s32[16,8]{0,1:T(8,128)S(1)}, s32[16,8]{0,1:T(8,128)}, u32[]{:S(2)}) copy-start(s32[16,8]{0,1:T(8,128)} %param.11) | copy-start | bytes 1540
  2.0 14.7 %all-to-all-start = ((f32[32,2,256]{2,1,0:T(2,128)}), f32[32,2,256]{2,1,0:T(2,128)S(1)}, u32[]{:S(2)}, u32[]{:S(2)}) async-start(f32[32,2,256]{2,1,0:T(2,128)} %broadcast_in_dim.8), calls=%async_computation | async-start | bytes 131072 | tf_op jit(solution)/shard_map/all_to_all | solution.py:344
  9.4 1.0 %copy-start.2 = (f32[256,256]{1,0:T(8,128)S(1)}, f32[256,256]{1,0:T(8,128)}, u32[]{:S(2)}) copy-start(f32[256,256]{1,0:T(8,128)} %h_ref.5) | copy-start | bytes 786436
  10.3 6.4 %copy-start.3 = (f32[256,256]{1,0:T(8,128)S(1)}, f32[256,256]{1,0:T(8,128)}, u32[]{:S(2)}) copy-start(f32[256,256]{1,0:T(8,128)} %h_ref.5) | copy-start | bytes 786436
  24.3 1.6 %collective-permute-start = (f32[256,256]{1,0:T(8,128)S(1)}, f32[256,256]{1,0:T(8,128)S(1)}, u32[]{:S(2)}, u32[]{:S(2)}) collective-permute-start(f32[256,256]{1,0:T(8,128)S(1)} %get-tuple-element.19), channel_id=1, source_target_pairs={{0,1},{1,0},{2,3},{3,2},{4,5},{5,4},{6,7},{7,6},{8,9},{9,8},{10,11... | collective-permute-start | bytes 786440 | tf_op jit(solution)/shard_map/ppermute | solution.py:367
